TPU v7x, 256 devices: a whole 4x4x8 slice. The times are simulated.
256 devices in a mesh: gx: 4 (over y_lo, core), gy: 16 (over y_hi, z), gz: 4 (over x).
Axes of the slice: x: 4, y: 4 (y_hi: 2, y_lo: 2; y = y_hi * 2 + y_lo), z: 8, core: 2. Of those that a mesh axis runs over, the one named last changes fastest.
Arguments:
- adjoint: float32 [19, 32, 256, 512], P(None, 'gx', 'gy', 'gz'), may hold values from -6 to 6
- density: float32 [2, 32, 256, 512], P(None, 'gx', 'gy', 'gz'), may hold values from 0.8 to 1.2
- velocity: float32 [2, 3, 32, 256, 512], P(None, None, 'gx', 'gy', 'gz'), may hold values from -0.25 to 0.25
- pore_mask: int32 [32, 256, 512], P('gx', 'gy', 'gz'), may hold values from 0 to 1, as said below
Outputs:
- adjoint_out: float32 [19, 32, 256, 512], P(None, 'gx', 'gy', 'gz')
- sensitivity: float32 [32, 256, 512], P('gx', 'gy', 'gz')
Inputs may be any that keep to these rules, and one draw needn't show every extreme that they name: `pore_mask`: 1 marks a pore voxel and 0 a solid one.
All inputs are finite; a program needn't handle non-finite values.
Results may differ from a plain program's by a relative error of at most 0.00002.
Values sent between devices are 32-bit elements; how exact they have to be, the bound alone decides.
A program may use at most 128 MiB of HBM per device.

v0:
```python
import jax
import jax.numpy as jnp
from jax import lax
from jax.sharding import PartitionSpec as P

VELOCITIES = [
    (0, 0, 0),
    (1, 0, 0),
    (-1, 0, 0),
    (0, 1, 0),
    (0, -1, 0),
    (0, 0, 1),
    (0, 0, -1),
    (1, 1, 0),
    (-1, -1, 0),
    (1, -1, 0),
    (-1, 1, 0),
    (1, 0, 1),
    (-1, 0, -1),
    (1, 0, -1),
    (-1, 0, 1),
    (0, 1, 1),
    (0, -1, -1),
    (0, 1, -1),
    (0, -1, 1),
]
WEIGHTS = [1.0 / 3.0] + [1.0 / 18.0] * 6 + [1.0 / 36.0] * 12
OPPOSITE = [0, 2, 1, 4, 3, 6, 5, 8, 7, 10, 9, 12, 11, 14, 13, 16, 15, 18, 17]
OMEGA = 1.25


def with_halo(block, sides, width):
    for axis, dim in sides:
        count = lax.axis_size(axis)
        forward = [(i, i + 1) for i in range(count - 1)]
        backward = [(target, source) for source, target in forward]
        low = lax.ppermute(
            lax.slice_in_dim(block, block.shape[dim] - width, None, axis=dim), axis, forward
        )
        high = lax.ppermute(lax.slice_in_dim(block, 0, width, axis=dim), axis, backward)
        block = jnp.concatenate([low, block, high], axis=dim)
    return block


def collide(pulled, rho, speed, pores):
    ux, uy, uz = (speed[0], speed[1], speed[2])
    usq = ux * ux + uy * uy + uz * uz
    shapes = []
    moment = jnp.zeros_like(rho)
    vec_x = jnp.zeros_like(rho)
    vec_y = jnp.zeros_like(rho)
    vec_z = jnp.zeros_like(rho)
    for index in range(19):
        cx, cy, cz = VELOCITIES[index]
        weight = WEIGHTS[index]
        along = cx * ux + cy * uy + cz * uz
        shaped = weight * (1.0 + 3.0 * along + 4.5 * along * along - 1.5 * usq)
        shapes.append(shaped)
        moment = moment + pulled[index] * shaped
        common = pulled[index] * weight
        vec_x = vec_x + common * (3.0 * cx + 9.0 * along * cx - 3.0 * ux)
        vec_y = vec_y + common * (3.0 * cy + 9.0 * along * cy - 3.0 * uy)
        vec_z = vec_z + common * (3.0 * cz + 9.0 * along * cz - 3.0 * uz)
    fluid = pores > 0
    layers = []
    change = jnp.zeros_like(rho)
    for index in range(19):
        cx, cy, cz = VELOCITIES[index]
        project = vec_x * (cx - ux) + vec_y * (cy - uy) + vec_z * (cz - uz)
        collided = (1.0 - OMEGA) * pulled[index] + OMEGA * (moment + project) + (cx - ux) / rho
        layers.append(jnp.where(fluid, collided, pulled[OPPOSITE[index]]))
        change = change + (pulled[OPPOSITE[index]] - pulled[index]) * rho * shapes[index]
    return (jnp.stack(layers), jnp.where(fluid, change, 0.0))


def pull_from(padded, out_x, out_y, out_z):
    return jnp.stack(
        [
            padded[
                index,
                1 + VELOCITIES[index][0] : 1 + VELOCITIES[index][0] + out_x,
                1 + VELOCITIES[index][1] : 1 + VELOCITIES[index][1] + out_y,
                1 + VELOCITIES[index][2] : 1 + VELOCITIES[index][2] + out_z,
            ]
            for index in range(19)
        ]
    )


def shards(adjoint, density, velocity, pore_mask):
    field = adjoint
    total = jnp.zeros(pore_mask.shape, jnp.float32)
    ext_x, ext_y, ext_z = pore_mask.shape
    for level in (1, 0):
        padded = with_halo(field, (("gx", 1), ("gy", 2), ("gz", 3)), 1)
        pulled = pull_from(padded, ext_x, ext_y, ext_z)
        field, change = collide(pulled, density[level], velocity[level], pore_mask)
        total = total + change
    return (field, total)


def solution(mesh):
    placed = (
        P(None, "gx", "gy", "gz"),
        P(None, "gx", "gy", "gz"),
        P(None, None, "gx", "gy", "gz"),
        P("gx", "gy", "gz"),
    )
    return jax.shard_map(
        shards,
        mesh=mesh,
        in_specs=placed,
        out_specs=(P(None, "gx", "gy", "gz"), P("gx", "gy", "gz")),
        check_vma=False,
    )
```

profile of v0, /device:TPU:24, one launch (start us, length us, event | category | flops | bytes accessed | tf_op | source)
XLA Modules:
  0.0 97.3 jit_solution(1609920642336264970)
XLA Ops:
  1.7 1.9 %collective-permute-start.1 = (f32[19,1,16,128]{3,2,1,0:T(8,128)S(1)}, f32[19,1,16,128]{3,2,1,0:T(8,128)S(1)}, u32[]{:S(2)}, u32[]{:S(2)}) collective-permute-start(f32[19,1,16,128]{3,2,1,0:T(8,128)S(1)} %get-tuple-element.115), channel_id=1, source_target_pairs={{0,64},{64,128},{128,192},{1,65},{65,129},{129,193},{2,66},{66,130... | collective-permute-start | bytes 466952 | tf_op jit(solution)/shard_map/ppermute | solution.py:37
  3.6 3.6 %collective-permute-start = (f32[19,1,16,128]{3,2,1,0:T(8,128)S(1)}, f32[19,1,16,128]{3,2,1,0:T(8,128)S(1)}, u32[]{:S(2)}, u32[]{:S(2)}) collective-permute-start(f32[19,1,16,128]{3,2,1,0:T(8,128)S(1)} %get-tuple-element.116), channel_id=1, source_target_pairs={{64,0},{128,64},{192,128},{65,1},{129,65},{193,129},{66,2},{130,66... | collective-permute-start | bytes 466952 | tf_op jit(solution)/shard_map/ppermute | solution.py:40
  10.5 3.8 %collective-permute-start.3 = (f32[19,10,1,128]{3,2,1,0:T(1,128)S(1)}, f32[19,10,1,128]{3,2,1,0:T(1,128)S(1)}, u32[]{:S(2)}, u32[]{:S(2)}) collective-permute-start(f32[19,10,1,128]{3,2,1,0:T(1,128)S(1)} %get-tuple-element.111), channel_id=1, source_target_pairs={{0,4},{4,8},{8,12},{12,16},{16,20},{20,24},{24,28},{28,32},{32,36}... | collective-permute-start | bytes 291848 | tf_op jit(solution)/shard_map/ppermute | solution.py:37
  14.3 6.5 %collective-permute-start.2 = (f32[19,10,1,128]{3,2,1,0:T(1,128)S(1)}, f32[19,10,1,128]{3,2,1,0:T(1,128)S(1)}, u32[]{:S(2)}, u32[]{:S(2)}) collective-permute-start(f32[19,10,1,128]{3,2,1,0:T(1,128)S(1)} %get-tuple-element.112), channel_id=1, source_target_pairs={{4,0},{8,4},{12,8},{16,12},{20,16},{24,20},{28,24},{32,28},{36,32}... | collective-permute-start | bytes 291848 | tf_op jit(solution)/shard_map/ppermute | solution.py:40
  24.0 2.1 %fusion.320 = (f32[19,10,18,1]{3,2,1,0:T(8,128)}, f32[19,10,18,1]{3,2,1,0:T(8,128)S(1)}) fusion(f32[19,10,18,128]{3,2,1,0:T(8,128)S(1)} %pad_maximum_fusion), kind=kLoop, calls=%fused_computation.547 | loop fusion | bytes 54720 | tf_op jit(solution)/shard_map/slice | solution.py:38
  26.2 2.8 %copy.21 = f32[19,10,18,1]{0,3,2,1:T(1,128)S(1)} copy(f32[19,10,18,1]{3,2,1,0:T(8,128)} %get-tuple-element.107) | data formatting | bytes 27360 | tf_op jit(solution)/shard_map/slice | solution.py:38
  29.0 3.4 %collective-permute-start.5 = (f32[19,10,18,1]{0,3,2,1:T(1,128)S(1)}, f32[19,10,18,1]{0,3,2,1:T(1,128)S(1)}, u32[]{:S(2)}, u32[]{:S(2)}) collective-permute-start(f32[19,10,18,1]{0,3,2,1:T(1,128)S(1)} %copy.21), channel_id=1, source_target_pairs={{0,1},{1,2},{2,3},{4,5},{5,6},{6,7},{8,9},{9,10},{10,11},{12,13},{... | collective-permute-start | bytes 41048 | tf_op jit(solution)/shard_map/ppermute | solution.py:37
  34.8 3.1 %copy.22 = f32[19,10,18,1]{3,2,1,0:T(8,128)} copy(f32[19,10,18,1]{0,3,2,1:T(1,128)S(1)} %collective-permute-done.5) | data formatting | bytes 27360 | tf_op jit(solution)/shard_map/ppermute | solution.py:37
  37.9 2.1 %collective-permute-done.4 = f32[19,10,18,1]{0,3,2,1:T(1,128)S(1)} collective-permute-done((f32[19,10,18,1]{0,3,2,1:T(1,128)S(1)}, f32[19,10,18,1]{0,3,2,1:T(1,128)S(1)}, u32[]{:S(2)}, u32[]{:S(2)}) %collective-permute-start.4) | collective-permute-done | bytes 13712 | tf_op jit(solution)/shard_map/ppermute | solution.py:40
  40.0 3.0 %copy.20 = f32[19,10,18,1]{3,2,1,0:T(8,128)} copy(f32[19,10,18,1]{0,3,2,1:T(1,128)S(1)} %collective-permute-done.4) | data formatting | bytes 27360 | tf_op jit(solution)/shard_map/ppermute | solution.py:40
  43.0 3.6 %constant_dynamic-update-slice_fusion.21 = (f32[19,8,16,128]{3,2,1,0:T(8,128)S(1)}, f32[8,16,128]{2,1,0:T(8,128)}, f32[8,16,128]{2,1,0:T(8,128)S(1)}, f32[8,16,1...) fusion(f32[19,8,16,128]{3,2,1,0:T(8,128)} %param.4, ...), kind=kLoop, calls=%fused_computation.64 | loop fusion | flops 8536063 | bytes 10811392
  48.0 1.9 %collective-permute-start.7 = (f32[19,1,16,128]{3,2,1,0:T(8,128)S(1)}, f32[19,1,16,128]{3,2,1,0:T(8,128)S(1)}, u32[]{:S(2)}, u32[]{:S(2)}) collective-permute-start(f32[19,1,16,128]{3,2,1,0:T(8,128)S(1)} %get-tuple-element.113), channel_id=1, source_target_pairs={{0,64},{64,128},{128,192},{1,65},{65,129},{129,193},{2,66},{66,130... | collective-permute-start | bytes 466952 | tf_op jit(solution)/shard_map/ppermute | solution.py:37
  50.0 3.6 %collective-permute-start.6 = (f32[19,1,16,128]{3,2,1,0:T(8,128)S(1)}, f32[19,1,16,128]{3,2,1,0:T(8,128)S(1)}, u32[]{:S(2)}, u32[]{:S(2)}) collective-permute-start(f32[19,1,16,128]{3,2,1,0:T(8,128)S(1)} %get-tuple-element.114), channel_id=1, source_target_pairs={{64,0},{128,64},{192,128},{65,1},{129,65},{193,129},{66,2},{130,66... | collective-permute-start | bytes 466952 | tf_op jit(solution)/shard_map/ppermute | solution.py:40
  54.6 1.8 %collective-permute-done.6 = f32[19,1,16,128]{3,2,1,0:T(8,128)S(1)} collective-permute-done((f32[19,1,16,128]{3,2,1,0:T(8,128)S(1)}, f32[19,1,16,128]{3,2,1,0:T(8,128)S(1)}, u32[]{:S(2)}, u32[]{:S(2)}) %collective-permute-start.6) | collective-permute-done | bytes 155680 | tf_op jit(solution)/shard_map/ppermute | solution.py:40
  56.5 1.9 %collective-permute-start.9 = (f32[19,10,1,128]{3,2,1,0:T(1,128)S(1)}, f32[19,10,1,128]{3,2,1,0:T(1,128)S(1)}, u32[]{:S(2)}, u32[]{:S(2)}) collective-permute-start(f32[19,10,1,128]{3,2,1,0:T(1,128)S(1)} %get-tuple-element.109), channel_id=1, source_target_pairs={{0,4},{4,8},{8,12},{12,16},{16,20},{20,24},{24,28},{28,32},{32,36}... | collective-permute-start | bytes 291848 | tf_op jit(solution)/shard_map/ppermute | solution.py:37
  58.4 7.9 %collective-permute-start.8 = (f32[19,10,1,128]{3,2,1,0:T(1,128)S(1)}, f32[19,10,1,128]{3,2,1,0:T(1,128)S(1)}, u32[]{:S(2)}, u32[]{:S(2)}) collective-permute-start(f32[19,10,1,128]{3,2,1,0:T(1,128)S(1)} %get-tuple-element.110), channel_id=1, source_target_pairs={{4,0},{8,4},{12,8},{16,12},{20,16},{24,20},{28,24},{32,28},{36,32}... | collective-permute-start | bytes 291848 | tf_op jit(solution)/shard_map/ppermute | solution.py:40
  69.2 2.9 %fusion.319 = (f32[19,10,18,1]{3,2,1,0:T(8,128)}, f32[19,10,18,1]{3,2,1,0:T(8,128)}) fusion(f32[19,10,18,128]{3,2,1,0:T(8,128)S(1)} %pad_maximum_fusion.1), kind=kLoop, calls=%fused_computation.546 | loop fusion | bytes 54720 | tf_op jit(solution)/shard_map/slice | solution.py:38
  72.1 2.8 %copy.25 = f32[19,10,18,1]{0,3,2,1:T(1,128)S(1)} copy(f32[19,10,18,1]{3,2,1,0:T(8,128)} %get-tuple-element.105) | data formatting | bytes 27360 | tf_op jit(solution)/shard_map/slice | solution.py:38
  74.9 3.4 %collective-permute-start.11 = (f32[19,10,18,1]{0,3,2,1:T(1,128)S(1)}, f32[19,10,18,1]{0,3,2,1:T(1,128)S(1)}, u32[]{:S(2)}, u32[]{:S(2)}) collective-permute-start(f32[19,10,18,1]{0,3,2,1:T(1,128)S(1)} %copy.25), channel_id=1, source_target_pairs={{0,1},{1,2},{2,3},{4,5},{5,6},{6,7},{8,9},{9,10},{10,11},{12,13},{... | collective-permute-start | bytes 41048 | tf_op jit(solution)/shard_map/ppermute | solution.py:37
  78.3 2.8 %copy.23 = f32[19,10,18,1]{0,3,2,1:T(1,128)S(1)} copy(f32[19,10,18,1]{3,2,1,0:T(8,128)} %get-tuple-element.106) | data formatting | bytes 27360 | tf_op jit(solution)/shard_map/slice | solution.py:40
  82.5 3.1 %copy.26 = f32[19,10,18,1]{3,2,1,0:T(8,128)} copy(f32[19,10,18,1]{0,3,2,1:T(1,128)S(1)} %collective-permute-done.11) | data formatting | bytes 27360 | tf_op jit(solution)/shard_map/ppermute | solution.py:37
  85.7 1.8 %collective-permute-done.10 = f32[19,10,18,1]{0,3,2,1:T(1,128)S(1)} collective-permute-done((f32[19,10,18,1]{0,3,2,1:T(1,128)S(1)}, f32[19,10,18,1]{0,3,2,1:T(1,128)S(1)}, u32[]{:S(2)}, u32[]{:S(2)}) %collective-permute-start.10) | collective-permute-done | bytes 13712 | tf_op jit(solution)/shard_map/ppermute | solution.py:40
  87.5 3.0 %copy.24 = f32[19,10,18,1]{3,2,1,0:T(8,128)} copy(f32[19,10,18,1]{0,3,2,1:T(1,128)S(1)} %collective-permute-done.10) | data formatting | bytes 27360 | tf_op jit(solution)/shard_map/ppermute | solution.py:40
  90.7 3.7 %select_add_fusion = (f32[8,16,128]{2,1,0:T(8,128)}, f32[8,16,128]{2,1,0:T(8,128)S(1)}, f32[8,16,128]{2,1,0:T(8,128)S(1)}, f32[8,16,128]{2,1,0:T(8,128)S(1)}, f3...) fusion(pred[8,16,128]{2,1,0:T(8,128)(4,1)S(1)} %get-tuple-eleme, ...), kind=kLoop, calls=%fused_computation.491 | loop fusion | flops 9043968 | bytes 6054624 | tf_op jit(solution)/shard_map/add | solution.py:98
  (142 shorter events, 19.4 us)
Async XLA Ops:
  1.7 6.5 %collective-permute-start.1 = (f32[19,1,16,128]{3,2,1,0:T(8,128)S(1)}, f32[19,1,16,128]{3,2,1,0:T(8,128)S(1)}, u32[]{:S(2)}, u32[]{:S(2)}) collective-permute-start(f32[19,1,16,128]{3,2,1,0:T(8,128)S(1)} %get-tuple-element.115), channel_id=1, source_target_pairs={{0,64},{64,128},{128,192},{1,65},{65,129},{129,193},{2,66},{66,130... | collective-permute-start | bytes 466952 | tf_op jit(solution)/shard_map/ppermute | solution.py:37
  3.6 6.7 %collective-permute-start = (f32[19,1,16,128]{3,2,1,0:T(8,128)S(1)}, f32[19,1,16,128]{3,2,1,0:T(8,128)S(1)}, u32[]{:S(2)}, u32[]{:S(2)}) collective-permute-start(f32[19,1,16,128]{3,2,1,0:T(8,128)S(1)} %get-tuple-element.116), channel_id=1, source_target_pairs={{64,0},{128,64},{192,128},{65,1},{129,65},{193,129},{66,2},{130,66... | collective-permute-start | bytes 466952 | tf_op jit(solution)/shard_map/ppermute | solution.py:40
  10.3 11.2 %copy-start.35 = (f32[19,1,16,128]{3,2,1,0:T(8,128)}, f32[19,1,16,128]{3,2,1,0:T(8,128)S(1)}, u32[]{:S(2)}) copy-start(f32[19,1,16,128]{3,2,1,0:T(8,128)S(1)} %collective-permute-done) | copy-start | bytes 466948
  10.3 12.7 %copy-start = (f32[19,10,16,128]{3,2,1,0:T(8,128)}, f32[19,10,16,128]{3,2,1,0:T(8,128)S(1)}, u32[]{:S(2)}) copy-start(f32[19,10,16,128]{3,2,1,0:T(8,128)S(1)} %constant_dynamic-update-slice_fusion) | copy-start | bytes 4669444
  10.5 11.0 %collective-permute-start.3 = (f32[19,10,1,128]{3,2,1,0:T(1,128)S(1)}, f32[19,10,1,128]{3,2,1,0:T(1,128)S(1)}, u32[]{:S(2)}, u32[]{:S(2)}) collective-permute-start(f32[19,10,1,128]{3,2,1,0:T(1,128)S(1)} %get-tuple-element.111), channel_id=1, source_target_pairs={{0,4},{4,8},{8,12},{12,16},{16,20},{20,24},{24,28},{28,32},{32,36}... | collective-permute-start | bytes 291848 | tf_op jit(solution)/shard_map/ppermute | solution.py:37
  14.3 8.7 %collective-permute-start.2 = (f32[19,10,1,128]{3,2,1,0:T(1,128)S(1)}, f32[19,10,1,128]{3,2,1,0:T(1,128)S(1)}, u32[]{:S(2)}, u32[]{:S(2)}) collective-permute-start(f32[19,10,1,128]{3,2,1,0:T(1,128)S(1)} %get-tuple-element.112), channel_id=1, source_target_pairs={{4,0},{8,4},{12,8},{16,12},{20,16},{24,20},{28,24},{32,28},{36,32}... | collective-permute-start | bytes 291848 | tf_op jit(solution)/shard_map/ppermute | solution.py:40
  29.0 5.9 %collective-permute-start.5 = (f32[19,10,18,1]{0,3,2,1:T(1,128)S(1)}, f32[19,10,18,1]{0,3,2,1:T(1,128)S(1)}, u32[]{:S(2)}, u32[]{:S(2)}) collective-permute-start(f32[19,10,18,1]{0,3,2,1:T(1,128)S(1)} %copy.21), channel_id=1, source_target_pairs={{0,1},{1,2},{2,3},{4,5},{5,6},{6,7},{8,9},{9,10},{10,11},{12,13},{... | collective-permute-start | bytes 41048 | tf_op jit(solution)/shard_map/ppermute | solution.py:37
  33.5 6.4 %collective-permute-start.4 = (f32[19,10,18,1]{0,3,2,1:T(1,128)S(1)}, f32[19,10,18,1]{0,3,2,1:T(1,128)S(1)}, u32[]{:S(2)}, u32[]{:S(2)}) collective-permute-start(f32[19,10,18,1]{0,3,2,1:T(1,128)S(1)} %copy.19), channel_id=1, source_target_pairs={{1,0},{2,1},{3,2},{5,4},{6,5},{7,6},{9,8},{10,9},{11,10},{13,12},{... | collective-permute-start | bytes 41048 | tf_op jit(solution)/shard_map/ppermute | solution.py:40
  37.9 5.1 %copy-start.1 = (f32[19,10,16,128]{3,2,1,0:T(8,128)S(1)}, f32[19,10,16,128]{3,2,1,0:T(8,128)}, u32[]{:S(2)}) copy-start(f32[19,10,16,128]{3,2,1,0:T(8,128)} %copy-done) | copy-start | bytes 4669444
  37.9 5.1 %copy-start.2 = (f32[2,3,8,16,128]{4,3,2,1,0:T(8,128)S(1)}, f32[2,3,8,16,128]{4,3,2,1,0:T(8,128)}, u32[]{:S(2)}) copy-start(f32[2,3,8,16,128]{4,3,2,1,0:T(8,128)} %param.6) | copy-start | bytes 1179652
  37.9 5.1 %copy-start.3 = (f32[2,8,16,128]{3,2,1,0:T(8,128)S(1)}, f32[2,8,16,128]{3,2,1,0:T(8,128)}, u32[]{:S(2)}) copy-start(f32[2,8,16,128]{3,2,1,0:T(8,128)} %param.5) | copy-start | bytes 393220
  48.0 6.5 %collective-permute-start.7 = (f32[19,1,16,128]{3,2,1,0:T(8,128)S(1)}, f32[19,1,16,128]{3,2,1,0:T(8,128)S(1)}, u32[]{:S(2)}, u32[]{:S(2)}) collective-permute-start(f32[19,1,16,128]{3,2,1,0:T(8,128)S(1)} %get-tuple-element.113), channel_id=1, source_target_pairs={{0,64},{64,128},{128,192},{1,65},{65,129},{129,193},{2,66},{66,130... | collective-permute-start | bytes 466952 | tf_op jit(solution)/shard_map/ppermute | solution.py:37
  50.0 6.4 %collective-permute-start.6 = (f32[19,1,16,128]{3,2,1,0:T(8,128)S(1)}, f32[19,1,16,128]{3,2,1,0:T(8,128)S(1)}, u32[]{:S(2)}, u32[]{:S(2)}) collective-permute-start(f32[19,1,16,128]{3,2,1,0:T(8,128)S(1)} %get-tuple-element.114), channel_id=1, source_target_pairs={{64,0},{128,64},{192,128},{65,1},{129,65},{193,129},{66,2},{130,66... | collective-permute-start | bytes 466952 | tf_op jit(solution)/shard_map/ppermute | solution.py:40
  56.5 10.5 %collective-permute-start.9 = (f32[19,10,1,128]{3,2,1,0:T(1,128)S(1)}, f32[19,10,1,128]{3,2,1,0:T(1,128)S(1)}, u32[]{:S(2)}, u32[]{:S(2)}) collective-permute-start(f32[19,10,1,128]{3,2,1,0:T(1,128)S(1)} %get-tuple-element.109), channel_id=1, source_target_pairs={{0,4},{4,8},{8,12},{12,16},{16,20},{20,24},{24,28},{28,32},{32,36}... | collective-permute-start | bytes 291848 | tf_op jit(solution)/shard_map/ppermute | solution.py:37
  58.4 10.1 %collective-permute-start.8 = (f32[19,10,1,128]{3,2,1,0:T(1,128)S(1)}, f32[19,10,1,128]{3,2,1,0:T(1,128)S(1)}, u32[]{:S(2)}, u32[]{:S(2)}) collective-permute-start(f32[19,10,1,128]{3,2,1,0:T(1,128)S(1)} %get-tuple-element.110), channel_id=1, source_target_pairs={{4,0},{8,4},{12,8},{16,12},{20,16},{24,20},{28,24},{32,28},{36,32}... | collective-permute-start | bytes 291848 | tf_op jit(solution)/shard_map/ppermute | solution.py:40
  74.9 7.7 %collective-permute-start.11 = (f32[19,10,18,1]{0,3,2,1:T(1,128)S(1)}, f32[19,10,18,1]{0,3,2,1:T(1,128)S(1)}, u32[]{:S(2)}, u32[]{:S(2)}) collective-permute-start(f32[19,10,18,1]{0,3,2,1:T(1,128)S(1)} %copy.25), channel_id=1, source_target_pairs={{0,1},{1,2},{2,3},{4,5},{5,6},{6,7},{8,9},{9,10},{10,11},{12,13},{... | collective-permute-start | bytes 41048 | tf_op jit(solution)/shard_map/ppermute | solution.py:37
  81.1 6.4 %collective-permute-start.10 = (f32[19,10,18,1]{0,3,2,1:T(1,128)S(1)}, f32[19,10,18,1]{0,3,2,1:T(1,128)S(1)}, u32[]{:S(2)}, u32[]{:S(2)}) collective-permute-start(f32[19,10,18,1]{0,3,2,1:T(1,128)S(1)} %copy.23), channel_id=1, source_target_pairs={{1,0},{2,1},{3,2},{5,4},{6,5},{7,6},{9,8},{10,9},{11,10},{13,12},{... | collective-permute-start | bytes 41048 | tf_op jit(solution)/shard_map/ppermute | solution.py:40
  85.6 4.9 %copy-start.13 = (f32[8,16,128]{2,1,0:T(8,128)S(1)}, f32[8,16,128]{2,1,0:T(8,128)}, u32[]{:S(2)}) copy-start(f32[8,16,128]{2,1,0:T(8,128)} %copy-done.12) | copy-start | bytes 196612
  85.6 4.9 %copy-start.15 = (f32[8,16,128]{2,1,0:T(8,128)S(1)}, f32[8,16,128]{2,1,0:T(8,128)}, u32[]{:S(2)}) copy-start(f32[8,16,128]{2,1,0:T(8,128)} %copy-done.14) | copy-start | bytes 196612
  85.6 4.9 %copy-start.17 = (f32[8,16,128]{2,1,0:T(8,128)S(1)}, f32[8,16,128]{2,1,0:T(8,128)}, u32[]{:S(2)}) copy-start(f32[8,16,128]{2,1,0:T(8,128)} %copy-done.16) | copy-start | bytes 196612
  85.7 4.9 %copy-start.19 = (f32[8,16,128]{2,1,0:T(8,128)S(1)}, f32[8,16,128]{2,1,0:T(8,128)}, u32[]{:S(2)}) copy-start(f32[8,16,128]{2,1,0:T(8,128)} %copy-done.18) | copy-start | bytes 196612
  85.7 4.9 %copy-start.21 = (f32[8,16,128]{2,1,0:T(8,128)S(1)}, f32[8,16,128]{2,1,0:T(8,128)}, u32[]{:S(2)}) copy-start(f32[8,16,128]{2,1,0:T(8,128)} %copy-done.20) | copy-start | bytes 196612
  85.7 4.9 %copy-start.23 = (f32[8,16,128]{2,1,0:T(8,128)S(1)}, f32[8,16,128]{2,1,0:T(8,128)}, u32[]{:S(2)}) copy-start(f32[8,16,128]{2,1,0:T(8,128)} %copy-done.22) | copy-start | bytes 196612
  85.7 4.9 %copy-start.25 = (f32[8,16,128]{2,1,0:T(8,128)S(1)}, f32[8,16,128]{2,1,0:T(8,128)}, u32[]{:S(2)}) copy-start(f32[8,16,128]{2,1,0:T(8,128)} %copy-done.24) | copy-start | bytes 196612
  (30 other events, 63.3 us)
where the time goes:
time: 98 us; the launch traced here: 97.3 us
  starting transfers between devices  40.9 us (42%)
  local copies, waits for them, and re-layouts  32.4 us (33%)
  waiting for transfers between devices  11.9 us (12%)
  other arithmetic  10.8 us (11%)
  between operations  1.36 us (1%)
    ppermute x6, starting transfers between devices, with_halo(): lax.ppermute(lax.slice_in_dim(block, 0, width, axis=dim), axis, backward)  24.5 us
    ppermute x6, starting transfers between devices, with_halo(): lax.ppermute(lax.slice_in_dim(block, block.shape[dim] - width, None, axis...  16.4 us
    slice x7, local copies, waits for them, and re-layouts, with_halo(): lax.slice_in_dim(block, block.shape[dim] - width, None, axis=dim)  11.8 us
    ppermute x6, waiting for transfers between devices, with_halo(): lax.ppermute(lax.slice_in_dim(block, 0, width, axis=dim), axis, backward)  8.67 us
    unnamed x36, other arithmetic  6.17 us
    ppermute x2, local copies, waits for them, and re-layouts, with_halo(): lax.ppermute(lax.slice_in_dim(block, block.shape[dim] - width, None, axis...  6.13 us
    ppermute x2, local copies, waits for them, and re-layouts, with_halo(): lax.ppermute(lax.slice_in_dim(block, 0, width, axis=dim), axis, backward)  6.07 us
    unnamed x86, local copies, waits for them, and re-layouts  4.45 us
  transfers between devices with their start and end apart: 12, of which 9 were waited for; matrix products, arithmetic and copies ran while one was open for 12% of the time, Pallas kernels for 0%

commit v1 on v0

v1 whole, which is shorter than its diff:
```python
import functools

import jax
import jax.numpy as jnp
from jax import lax
from jax.experimental import pallas as pl
from jax.experimental.pallas import tpu as pltpu
from jax.sharding import PartitionSpec as P

VELOCITIES = [
    (0, 0, 0),
    (1, 0, 0),
    (-1, 0, 0),
    (0, 1, 0),
    (0, -1, 0),
    (0, 0, 1),
    (0, 0, -1),
    (1, 1, 0),
    (-1, -1, 0),
    (1, -1, 0),
    (-1, 1, 0),
    (1, 0, 1),
    (-1, 0, -1),
    (1, 0, -1),
    (-1, 0, 1),
    (0, 1, 1),
    (0, -1, -1),
    (0, 1, -1),
    (0, -1, 1),
]
WEIGHTS = [1.0 / 3.0] + [1.0 / 18.0] * 6 + [1.0 / 36.0] * 12
OPPOSITE = [0, 2, 1, 4, 3, 6, 5, 8, 7, 10, 9, 12, 11, 14, 13, 16, 15, 18, 17]
OMEGA = 1.25
MESH = pl.DeviceIdType.MESH

CXP = [1, 7, 9, 11, 13]
CXM = [2, 8, 10, 12, 14]
CYP = [3, 7, 10, 15, 17]
CYM = [4, 8, 9, 16, 18]
ZCOLS = [(5, 0), (11, 0), (14, 0), (15, 0), (18, 0), (6, -1), (12, -1), (13, -1), (16, -1), (17, -1)]
ZFACE_COL = {5: 0, 11: 8, 14: 16, 15: 24, 18: 32, 6: 0, 12: 8, 13: 16, 16: 24, 17: 32}
XZ_EDGE = {11: (40, 0), 14: (48, -16), 12: (40, -16), 13: (48, 0)}
YZ_CORNER = {15: (56, 0), 18: (64, -1), 16: (56, -1), 17: (64, 0)}
XY_EDGE = {7: (0, 0), 8: (1, 7), 9: (2, 7), 10: (3, 0)}


def _messages(cx, cy):
    rows = cx * cy
    msgs = []
    for k, pop in enumerate(CXP):
        msgs.append(((-1, 0, 0), ("S", pop, 0, cy), ("XH", 1, k)))
    for k, pop in enumerate(CXM):
        msgs.append(((1, 0, 0), ("S", pop, rows - cy, cy), ("XH", 0, k)))
    msgs.append(((0, -1, 0), ("SY", 0), ("YH", 1)))
    msgs.append(((0, 1, 0), ("SY", 1), ("YH", 0)))
    msgs.append(((-1, -1, 0), ("S", 7, 0, 8), ("EXY", 0)))
    msgs.append(((1, 1, 0), ("S", 8, rows - 8, 8), ("EXY", 1)))
    msgs.append(((-1, 1, 0), ("S", 9, cy - 8, 8), ("EXY", 2)))
    msgs.append(((1, -1, 0), ("S", 10, rows - cy, 8), ("EXY", 3)))
    msgs.append(((0, 0, -1), ("NT", 0, 40), ("MH", 1, 0, 40)))
    msgs.append(((0, 0, 1), ("NT", 40, 40), ("MH", 0, 0, 40)))
    msgs.append(((-1, 0, -1), ("NT", 8, 8), ("MH", 1, 40, 8)))
    msgs.append(((1, 0, -1), ("NT", 16, 8), ("MH", 1, 48, 8)))
    msgs.append(((1, 0, 1), ("NT", 48, 8), ("MH", 0, 40, 8)))
    msgs.append(((-1, 0, 1), ("NT", 56, 8), ("MH", 0, 48, 8)))
    msgs.append(((0, -1, -1), ("NT", 24, 8), ("MH", 1, 56, 8)))
    msgs.append(((0, 1, -1), ("NT", 32, 8), ("MH", 1, 64, 8)))
    msgs.append(((0, 1, 1), ("NT", 64, 8), ("MH", 0, 56, 8)))
    msgs.append(((0, -1, 1), ("NT", 72, 8), ("MH", 0, 64, 8)))
    return msgs


NEIGHBOURS = sorted(
    {d for d, _, _ in _messages(8, 16)} | {tuple(-v for v in d) for d, _, _ in _messages(8, 16)}
)


def _comb(vals, fn):
    total = None
    for weight in (1.0 / 3.0, 1.0 / 18.0, 1.0 / 36.0):
        part = None
        for i in range(19):
            if WEIGHTS[i] != weight:
                continue
            k = fn(VELOCITIES[i])
            if k == 0:
                continue
            if part is None:
                part = vals[i] if k > 0 else -vals[i]
            else:
                part = part + vals[i] if k > 0 else part - vals[i]
        if part is not None:
            term = part * weight
            total = term if total is None else total + term
    return total


def _collide(pulled, rho, ux, uy, uz, fluid):
    p0 = _comb(pulled, lambda c: 1)
    p1 = [_comb(pulled, lambda c, a=a: c[a]) for a in range(3)]
    q = {}
    for a in range(3):
        for b in range(a, 3):
            q[a, b] = _comb(pulled, lambda c, a=a, b=b: c[a] * c[b])
            q[b, a] = q[a, b]
    u = (ux, uy, uz)
    usq = ux * ux + uy * uy + uz * uz
    qu = [q[a, 0] * ux + q[a, 1] * uy + q[a, 2] * uz for a in range(3)]
    p1u = p1[0] * ux + p1[1] * uy + p1[2] * uz
    uqu = ux * qu[0] + uy * qu[1] + uz * qu[2]
    moment = p0 * (1.0 - 1.5 * usq) + 3.0 * p1u + 4.5 * uqu
    vec = [3.0 * p1[a] + 9.0 * qu[a] - 3.0 * u[a] * p0 for a in range(3)]
    vu = vec[0] * ux + vec[1] * uy + vec[2] * uz
    inv = 1.0 / rho
    base = OMEGA * (moment - vu) - ux * inv
    bases = {0: base, 1: base + inv, -1: base - inv}
    wv = [OMEGA * v for v in vec]
    combos = {}
    layers = []
    for i in range(19):
        c = VELOCITIES[i]
        key = tuple(c)
        terms = [(a, c[a]) for a in range(3) if c[a] != 0]
        cv = None
        if terms:
            if len(terms) == 1:
                a, s = terms[0]
                cv = wv[a] if s > 0 else -wv[a]
            else:
                (a, s), (b, t) = terms
                pos = (a, b, s * t)
                if pos not in combos:
                    combos[pos] = wv[a] + wv[b] if s * t > 0 else wv[a] - wv[b]
                cv = combos[pos] if s > 0 else -combos[pos]
        val = (1.0 - OMEGA) * pulled[i] + bases[c[0]]
        if cv is not None:
            val = val + cv
        layers.append(jnp.where(fluid, val, pulled[OPPOSITE[i]]))
    sens = None
    for i in range(1, 19, 2):
        c = VELOCITIES[i]
        along = None
        for a in range(3):
            if c[a] == 0:
                continue
            if along is None:
                along = u[a] if c[a] > 0 else -u[a]
            else:
                along = along + u[a] if c[a] > 0 else along - u[a]
        term = (6.0 * WEIGHTS[i]) * along * (pulled[OPPOSITE[i]] - pulled[i])
        sens = term if sens is None else sens + term
    sens = jnp.where(fluid, rho * sens, 0.0)
    return layers, sens


def _kernel(dims, adj_ref, rho_ref, vel_ref, mask_ref, out_ref, sens_ref,
            mid, xh, yh, exy, sy, nt, mh, mt, send_sem, recv_sem):
    nx, ny, nz = dims
    cx, cy, cz = 8, 16, 128
    rows = cx * cy
    me = (lax.axis_index("gx"), lax.axis_index("gy"), lax.axis_index("gz"))
    sizes = (nx, ny, nz)

    def exists(d):
        cond = None
        for a in range(3):
            if d[a] == 0:
                continue
            v = me[a] + d[a]
            c = (v >= 0) if d[a] < 0 else (v < sizes[a])
            cond = c if cond is None else jnp.logical_and(cond, c)
        return cond

    def target(d):
        return tuple(me[a] + d[a] for a in range(3))

    xh[...] = jnp.zeros(xh.shape, jnp.float32)
    yh[...] = jnp.zeros(yh.shape, jnp.float32)
    exy[...] = jnp.zeros(exy.shape, jnp.float32)
    mh[...] = jnp.zeros(mh.shape, jnp.float32)

    barrier = pltpu.get_barrier_semaphore()
    for d in NEIGHBOURS:
        @pl.when(exists(d))
        def _():
            pl.semaphore_signal(barrier, inc=1, device_id=target(d), device_id_type=MESH)

    lane = lax.broadcasted_iota(jnp.int32, (cy, cz), 1)
    lane1 = lax.broadcasted_iota(jnp.int32, (1, cz), 1)
    row = lax.broadcasted_iota(jnp.int32, (cy, cz), 0)
    lane_big = lax.broadcasted_iota(jnp.int32, (rows, cz), 1)

    msgs = _messages(cx, cy)

    def prepare(s, src):
        for side, pops, y in ((0, CYP, 0), (1, CYM, cy - 1)):
            for k, pop in enumerate(pops):
                sy[s, side, k] = src[pop, pl.ds(y, cx, stride=cy), :]
        n = jnp.zeros((rows, cz), jnp.float32)
        for j, (pop, z) in enumerate(ZCOLS):
            zz = z % cz
            n = jnp.where(lane_big == 8 * j, pltpu.roll(src[pop], (8 * j - zz) % cz, 1), n)
        nt[s] = n.T

    def descriptor(s, src, m, t):
        d, so, de = msgs[t]
        if so[0] == "S":
            sref = src.at[so[1], pl.ds(so[2] % rows, so[3]), :]
        elif so[0] == "SY":
            sref = sy.at[s, so[1]]
        else:
            sref = nt.at[s, pl.ds(so[1], so[2]), :]
        if de[0] == "XH":
            dref = xh.at[s, de[1], de[2]]
        elif de[0] == "YH":
            dref = yh.at[s, de[1]]
        elif de[0] == "EXY":
            dref = exy.at[s, de[1]]
        else:
            dref = mh.at[s, de[1], pl.ds(de[2], de[3]), :]
        return pltpu.make_async_remote_copy(
            src_ref=sref, dst_ref=dref, send_sem=send_sem.at[s, t], recv_sem=recv_sem.at[s, t],
            device_id=target(d), device_id_type=MESH)

    def send(s, src):
        for t in range(len(msgs)):
            d = msgs[t][0]

            @pl.when(exists(d))
            def _():
                descriptor(s, src, msgs, t).start()

    def finish(s, src):
        for t in range(len(msgs)):
            d = msgs[t][0]
            back = tuple(-v for v in d)

            @pl.when(exists(back))
            def _():
                descriptor(s, src, msgs, t).wait_recv()

            @pl.when(exists(d))
            def _():
                descriptor(s, src, msgs, t).wait_send()
        for side in range(2):
            mt[s, side] = mh[s, side].T

    def pulled_plane(s, src, p):
        out = []
        for i in range(19):
            vx, vy, vz = VELOCITIES[i]
            q = p + vx
            if 0 <= q < cx:
                plane = src[i, pl.ds(q * cy, cy), :]
            elif q == cx:
                plane = xh[s, 1, CXP.index(i)]
            else:
                plane = xh[s, 0, CXM.index(i)]
            if vz != 0:
                side = 1 if vz > 0 else 0
                if 0 <= q < cx:
                    zc = mt[s, side, pl.ds(q * cy, cy), :]
                    col = ZFACE_COL[i]
                else:
                    col, r0 = XZ_EDGE[i]
                    zc = mt[s, side, pl.ds(r0 % rows, cy), :]
                if vz > 0:
                    plane = jnp.where(lane == cz - 1, pltpu.roll(zc, (cz - 1 - col) % cz, 1),
                                      pltpu.roll(plane, cz - 1, 1))
                else:
                    plane = jnp.where(lane == 0, pltpu.roll(zc, (cz - col) % cz, 1),
                                      pltpu.roll(plane, 1, 1))
            if vy != 0:
                side_y = 1 if vy > 0 else 0
                ky = CYP.index(i) if vy > 0 else CYM.index(i)
                if 0 <= q < cx:
                    yrow = yh[s, side_y, ky, pl.ds(q, 1), :]
                else:
                    e, r = XY_EDGE[i]
                    yrow = exy[s, e, pl.ds(r, 1), :]
                if vz != 0:
                    side = 1 if vz > 0 else 0
                    colc, yoff = YZ_CORNER[i]
                    crow = mt[s, side, pl.ds(p * cy + yoff % cy, 1), :]
                    if vz > 0:
                        yrow = jnp.where(lane1 == cz - 1, pltpu.roll(crow, (cz - 1 - colc) % cz, 1),
                                         pltpu.roll(yrow, cz - 1, 1))
                    else:
                        yrow = jnp.where(lane1 == 0, pltpu.roll(crow, (cz - colc) % cz, 1),
                                         pltpu.roll(yrow, 1, 1))
                if vy > 0:
                    plane = jnp.where(row == cy - 1, yrow, pltpu.roll(plane, cy - 1, 0))
                else:
                    plane = jnp.where(row == 0, yrow, pltpu.roll(plane, 1, 0))
            out.append(plane)
        return out

    def step(s, src, dst, level):
        for p in range(cx):
            rs = pl.ds(p * cy, cy)
            pulled = pulled_plane(s, src, p)
            rho = rho_ref[level, rs, :]
            ux = vel_ref[level, 0, rs, :]
            uy = vel_ref[level, 1, rs, :]
            uz = vel_ref[level, 2, rs, :]
            fluid = mask_ref[rs, :] > 0
            layers, sens = _collide(pulled, rho, ux, uy, uz, fluid)
            for i in range(19):
                dst[i, rs, :] = layers[i]
            if s == 0:
                sens_ref[rs, :] = sens
            else:
                sens_ref[rs, :] = sens_ref[rs, :] + sens

    def indicator(a, off):
        n = sizes[a]
        if off < 0:
            return (me[a] + n - 1) // n
        if off > 0:
            return (2 * n - 2 - me[a]) // n
        return 1

    peers = 0
    for d in NEIGHBOURS:
        term = 1
        for a in range(3):
            term = term * indicator(a, d[a])
        peers = peers + term
    prepare(0, adj_ref)
    pl.semaphore_wait(barrier, peers)
    send(0, adj_ref)
    finish(0, adj_ref)
    step(0, adj_ref, mid, 1)
    prepare(1, mid)
    send(1, mid)
    finish(1, mid)
    step(1, mid, out_ref, 0)


def solution(mesh):
    nx, ny, nz = mesh.shape["gx"], mesh.shape["gy"], mesh.shape["gz"]
    nmsg = len(_messages(8, 16))

    def shards(adjoint, density, velocity, pore_mask):
        npop, cx, cy, cz = adjoint.shape
        assert (cx, cy, cz) == (8, 16, 128)
        rows = cx * cy
        adj = adjoint.reshape(npop, rows, cz)
        rho = density.reshape(2, rows, cz)
        vel = velocity.reshape(2, 3, rows, cz)
        mask = pore_mask.reshape(rows, cz)
        vspec = pl.BlockSpec(memory_space=pltpu.VMEM)
        out, sens = pl.pallas_call(
            functools.partial(_kernel, (nx, ny, nz)),
            out_shape=(
                jax.ShapeDtypeStruct((npop, rows, cz), jnp.float32),
                jax.ShapeDtypeStruct((rows, cz), jnp.float32),
            ),
            in_specs=[vspec] * 4,
            out_specs=(vspec, vspec),
            scratch_shapes=[
                pltpu.VMEM((npop, rows, cz), jnp.float32),
                pltpu.VMEM((2, 2, 5, cy, cz), jnp.float32),
                pltpu.VMEM((2, 2, 5, cx, cz), jnp.float32),
                pltpu.VMEM((2, 4, 8, cz), jnp.float32),
                pltpu.VMEM((2, 2, 5, cx, cz), jnp.float32),
                pltpu.VMEM((2, rows, cz), jnp.float32),
                pltpu.VMEM((2, 2, rows, cz), jnp.float32),
                pltpu.VMEM((2, 2, rows, cz), jnp.float32),
                pltpu.SemaphoreType.DMA((2, nmsg)),
                pltpu.SemaphoreType.DMA((2, nmsg)),
            ],
            compiler_params=pltpu.CompilerParams(
                collective_id=0, has_side_effects=True, vmem_limit_bytes=48 * 1024 * 1024
            ),
        )(adj, rho, vel, mask)
        return out.reshape(npop, cx, cy, cz), sens.reshape(cx, cy, cz)

    placed = (
        P(None, "gx", "gy", "gz"),
        P(None, "gx", "gy", "gz"),
        P(None, None, "gx", "gy", "gz"),
        P("gx", "gy", "gz"),
    )
    return jax.shard_map(
        shards,
        mesh=mesh,
        in_specs=placed,
        out_specs=(P(None, "gx", "gy", "gz"), P("gx", "gy", "gz")),
        check_vma=False,
    )
```

time: 98 us -> 28.3 us (0.29)
  starting transfers between devices: 40.9 us -> 0 us
  local copies, waits for them, and re-layouts: 32.4 us -> 5.69 us
  Pallas kernels: 0 us -> 21.7 us
  waiting for transfers between devices: 11.9 us -> 0 us
  other arithmetic: 10.8 us -> 0 us
    ppermute x12 -> x0, starting transfers between devices: 40.9 us -> none  [the longest x6 24.5 us: with_halo(): lax.ppermute(lax.slice_in_dim(block, 0, width, axis=dim), axis, backward)]
    pallas_call x0 -> x1, Pallas kernels: none -> 21.7 us  [shards(): pl.pallas_call(functools.partial(_kernel, (nx, ny, nz)), out_shape=(jax.S...]
    slice x9 -> x0, local copies, waits for them, and re-layouts: 15.8 us -> none  [the longest x7 11.8 us: with_halo(): lax.slice_in_dim(block, block.shape[dim] - width, None, axis=dim)]
    ppermute x4 -> x0, local copies, waits for them, and re-layouts: 12.2 us -> none  [the longest x2 6.13 us: with_halo(): lax.ppermute(lax.slice_in_dim(block, block.shape[dim] - width, None, axis...]
    ppermute x12 -> x0, waiting for transfers between devices: 11.9 us -> none  [the longest x6 8.67 us: with_halo(): lax.ppermute(lax.slice_in_dim(block, 0, width, axis=dim), axis, backward)]
    unnamed x36 -> x0, other arithmetic: 6.17 us -> none
    add x1 -> x0, other arithmetic: 3.69 us -> none  [shards(): total = total + change]
    unnamed x86 -> x10, local copies, waits for them, and re-layouts: 4.45 us -> 5.69 us
  transfers between devices with their start and end apart: 12 -> 0, of which waited for: 9 -> 0; matrix products, arithmetic and copies ran while one was open for 12% -> 0% of each run, Pallas kernels for 0% -> 0%
where the time goes in v1:
time: 28.3 us; the launch traced here: 28.1 us
  Pallas kernels  21.7 us (77%)
  local copies, waits for them, and re-layouts  5.69 us (20%)
  between operations  0.65 us (2%)
    pallas_call x1, Pallas kernels, shards(): pl.pallas_call(functools.partial(_kernel, (nx, ny, nz)), out_shape=(jax.S...  21.7 us
    unnamed x10, local copies, waits for them, and re-layouts  5.69 us

profile of v1, /device:TPU:24, one launch (start us, length us, event | category | flops | bytes accessed | tf_op | source)
XLA Modules:
  0.0 28.1 jit_solution(5921842324475405783)
XLA Ops:
  0.6 0.0 copy-start
  0.6 1.3 %copy-done = f32[19,8,16,128]{3,2,1,0:T(8,128)S(1)} copy-done((f32[19,8,16,128]{3,2,1,0:T(8,128)S(1)}, f32[19,8,16,128]{3,2,1,0:T(8,128)}, u32[]{:S(2)}) %copy-start) | copy-done | bytes 1245208
  1.9 0.0 copy-start.1
  1.9 1.0 %copy-done.1 = f32[2,3,8,16,128]{4,3,2,1,0:T(8,128)S(1)} copy-done((f32[2,3,8,16,128]{4,3,2,1,0:T(8,128)S(1)}, f32[2,3,8,16,128]{4,3,2,1,0:T(8,128)}, u32[]{:S(2)}) %copy-start.1) | copy-done | bytes 393240
  2.9 0.0 copy-start.2
  2.9 0.9 %copy-done.2 = f32[2,8,16,128]{3,2,1,0:T(8,128)S(1)} copy-done((f32[2,8,16,128]{3,2,1,0:T(8,128)S(1)}, f32[2,8,16,128]{3,2,1,0:T(8,128)}, u32[]{:S(2)}) %copy-start.2) | copy-done | bytes 131096
  3.8 0.0 copy-start.3
  3.8 0.8 %copy-done.3 = s32[8,16,128]{2,1,0:T(8,128)S(1)} copy-done((s32[8,16,128]{2,1,0:T(8,128)S(1)}, s32[8,16,128]{2,1,0:T(8,128)}, u32[]{:S(2)}) %copy-start.3) | copy-done | bytes 65560
  4.7 21.7 %shard_map.59 = (f32[19,128,128]{2,1,0:T(8,128)S(1)}, f32[128,128]{1,0:T(8,128)S(1)}) custom-call(f32[19,128,128]{2,1,0:T(8,128)S(1)} %bitcast.6, f32[2,128,128]{2,1,0:T(8,128)S(1)} %bitcast.9, f32[2,3,128,128]{3,2,1,0:T(8,128)S(1)} %bitcast.8, s32[128,128]{1,0:T(8,128)S(1)} %bitcast.10), custom_call_target="tpu_custom_call" | custom-call | tf_op jit(solution)/shard_map/pallas_call | solution.py:353
  26.4 1.0 %copy.8 = f32[19,8,16,128]{3,2,1,0:T(8,128)} copy(f32[19,8,16,128]{3,2,1,0:T(8,128)S(1)} %bitcast.7) | data formatting | bytes 2490368
  27.4 0.6 %copy.9 = f32[8,16,128]{2,1,0:T(8,128)} copy(f32[8,16,128]{2,1,0:T(8,128)S(1)} %bitcast.11) | data formatting | bytes 131072
Async XLA Ops:
  0.6 1.3 %copy-start = (f32[19,8,16,128]{3,2,1,0:T(8,128)S(1)}, f32[19,8,16,128]{3,2,1,0:T(8,128)}, u32[]{:S(2)}) copy-start(f32[19,8,16,128]{3,2,1,0:T(8,128)} %param.4) | copy-start | bytes 3735556
  1.9 1.0 %copy-start.1 = (f32[2,3,8,16,128]{4,3,2,1,0:T(8,128)S(1)}, f32[2,3,8,16,128]{4,3,2,1,0:T(8,128)}, u32[]{:S(2)}) copy-start(f32[2,3,8,16,128]{4,3,2,1,0:T(8,128)} %param.6) | copy-start | bytes 1179652
  2.9 0.9 %copy-start.2 = (f32[2,8,16,128]{3,2,1,0:T(8,128)S(1)}, f32[2,8,16,128]{3,2,1,0:T(8,128)}, u32[]{:S(2)}) copy-start(f32[2,8,16,128]{3,2,1,0:T(8,128)} %param.5) | copy-start | bytes 393220
  3.8 0.8 %copy-start.3 = (s32[8,16,128]{2,1,0:T(8,128)S(1)}, s32[8,16,128]{2,1,0:T(8,128)}, u32[]{:S(2)}) copy-start(s32[8,16,128]{2,1,0:T(8,128)} %param.7) | copy-start | bytes 196612

commit v2 on v1

--- a/solution.py
+++ b/solution.py
@@ -153,7 +153,8 @@
     return layers, sens
 
 
-def _kernel(dims, adj_ref, rho_ref, vel_ref, mask_ref, out_ref, sens_ref,
+def _kernel(dims, adj_hbm, rho_hbm, vel_hbm, mask_hbm, out_ref, sens_ref,
+            adj_ref, rho_ref, vel_ref, mask_ref, load_sem,
             mid, xh, yh, exy, sy, nt, mh, mt, send_sem, recv_sem):
     nx, ny, nz = dims
     cx, cy, cz = 8, 16, 128
@@ -173,6 +174,15 @@
 
     def target(d):
         return tuple(me[a] + d[a] for a in range(3))
+
+    loads = [
+        pltpu.make_async_copy(src, dst, load_sem.at[k])
+        for k, (src, dst) in enumerate(
+            ((adj_hbm, adj_ref), (vel_hbm, vel_ref), (rho_hbm, rho_ref), (mask_hbm, mask_ref))
+        )
+    ]
+    for copy in loads:
+        copy.start()
 
     xh[...] = jnp.zeros(xh.shape, jnp.float32)
     yh[...] = jnp.zeros(yh.shape, jnp.float32)
@@ -326,9 +336,12 @@
         for a in range(3):
             term = term * indicator(a, d[a])
         peers = peers + term
+    loads[0].wait()
     prepare(0, adj_ref)
     pl.semaphore_wait(barrier, peers)
     send(0, adj_ref)
+    for copy in loads[1:]:
+        copy.wait()
     finish(0, adj_ref)
     step(0, adj_ref, mid, 1)
     prepare(1, mid)
@@ -356,9 +369,14 @@
                 jax.ShapeDtypeStruct((npop, rows, cz), jnp.float32),
                 jax.ShapeDtypeStruct((rows, cz), jnp.float32),
             ),
-            in_specs=[vspec] * 4,
+            in_specs=[pl.BlockSpec(memory_space=pltpu.HBM)] * 4,
             out_specs=(vspec, vspec),
             scratch_shapes=[
+                pltpu.VMEM((npop, rows, cz), jnp.float32),
+                pltpu.VMEM((2, rows, cz), jnp.float32),
+                pltpu.VMEM((2, 3, rows, cz), jnp.float32),
+                pltpu.VMEM((rows, cz), jnp.int32),
+                pltpu.SemaphoreType.DMA((4,)),
                 pltpu.VMEM((npop, rows, cz), jnp.float32),
                 pltpu.VMEM((2, 2, 5, cy, cz), jnp.float32),
                 pltpu.VMEM((2, 2, 5, cx, cz), jnp.float32),
@@ -371,7 +389,7 @@
                 pltpu.SemaphoreType.DMA((2, nmsg)),
             ],
             compiler_params=pltpu.CompilerParams(
-                collective_id=0, has_side_effects=True, vmem_limit_bytes=48 * 1024 * 1024
+                collective_id=0, has_side_effects=True, vmem_limit_bytes=67043328
             ),
         )(adj, rho, vel, mask)
         return out.reshape(npop, cx, cy, cz), sens.reshape(cx, cy, cz)

time: 28.3 us -> 26.7 us (0.943)
  local copies, waits for them, and re-layouts: 5.69 us -> 3.11 us
  Pallas kernels: 21.7 us -> 22.8 us
    unnamed x10 -> x4, local copies, waits for them, and re-layouts: 5.69 us -> 3.11 us
    pallas_call x1, Pallas kernels: 21.7 us -> 22.8 us  [shards(): pl.pallas_call(functools.partial(_kernel, (nx, ny, nz)), out_shape=(jax.S...]
where the time goes in v2:
time: 26.7 us; the launch traced here: 26.6 us
  Pallas kernels  22.8 us (85%)
  local copies, waits for them, and re-layouts  3.11 us (12%)
  between operations  0.65 us (2%)
    pallas_call x1, Pallas kernels, shards(): pl.pallas_call(functools.partial(_kernel, (nx, ny, nz)), out_shape=(jax.S...  22.8 us
    unnamed x4, local copies, waits for them, and re-layouts  3.11 us

profile of v2, /device:TPU:24, one launch (start us, length us, event | category | flops | bytes accessed | tf_op | source)
XLA Modules:
  0.0 26.6 jit_solution(11352140339247381053)
XLA Ops:
  0.6 22.8 %shard_map.59 = (f32[19,128,128]{2,1,0:T(8,128)}, f32[128,128]{1,0:T(8,128)}) custom-call(f32[19,128,128]{2,1,0:T(8,128)} %bitcast.6, f32[2,128,128]{2,1,0:T(8,128)} %bitcast.9, f32[2,3,128,128]{3,2,1,0:T(8,128)} %bitcast.8, s32[128,128]{1,0:T(8,128)} %bitcast.10), custom_call_target="tpu_custom_call" | custom-call | tf_op jit(solution)/shard_map/pallas_call | solution.py:366
  23.5 0.0 copy-start
  23.5 2.5 %copy.8 = f32[19,8,16,128]{3,2,1,0:T(8,128)} copy(f32[19,8,16,128]{3,2,1,0:T(8,128)} %bitcast.7) | data formatting | bytes 2490368
  26.0 0.0 copy-done
  26.0 0.6 %copy.9 = f32[8,16,128]{2,1,0:T(8,128)} copy(f32[8,16,128]{2,1,0:T(8,128)S(1)} %bitcast.11) | data formatting | bytes 131072
Async XLA Ops:
  23.5 2.5 %copy-start = (f32[128,128]{1,0:T(8,128)S(1)}, f32[128,128]{1,0:T(8,128)}, u32[]{:S(2)}) copy-start(f32[128,128]{1,0:T(8,128)} %get-tuple-element.5) | copy-start | bytes 196612

commit v3 on v2

--- a/solution.py
+++ b/solution.py
@@ -95,7 +95,7 @@
     return total
 
 
-def _collide(pulled, rho, ux, uy, uz, fluid):
+def _collide(pulled, rho, ux, uy, uz, fluid, with_rho=True):
     p0 = _comb(pulled, lambda c: 1)
     p1 = [_comb(pulled, lambda c, a=a: c[a]) for a in range(3)]
     q = {}
@@ -111,9 +111,13 @@
     moment = p0 * (1.0 - 1.5 * usq) + 3.0 * p1u + 4.5 * uqu
     vec = [3.0 * p1[a] + 9.0 * qu[a] - 3.0 * u[a] * p0 for a in range(3)]
     vu = vec[0] * ux + vec[1] * uy + vec[2] * uz
-    inv = 1.0 / rho
-    base = OMEGA * (moment - vu) - ux * inv
-    bases = {0: base, 1: base + inv, -1: base - inv}
+    if with_rho:
+        inv = 1.0 / rho
+        base = OMEGA * (moment - vu) - ux * inv
+        bases = {0: base, 1: base + inv, -1: base - inv}
+    else:
+        base = OMEGA * (moment - vu)
+        bases = {0: base, 1: base, -1: base}
     wv = [OMEGA * v for v in vec]
     combos = {}
     layers = []
@@ -153,7 +157,7 @@
     return layers, sens
 
 
-def _kernel(dims, adj_hbm, rho_hbm, vel_hbm, mask_hbm, out_ref, sens_ref,
+def _kernel(dims, adj_hbm, rho_hbm, vel_hbm, mask_hbm, out_ref, sens_ref, sens2_ref,
             adj_ref, rho_ref, vel_ref, mask_ref, load_sem,
             mid, xh, yh, exy, sy, nt, mh, mt, send_sem, recv_sem):
     nx, ny, nz = dims
@@ -314,13 +318,13 @@
             uy = vel_ref[level, 1, rs, :]
             uz = vel_ref[level, 2, rs, :]
             fluid = mask_ref[rs, :] > 0
-            layers, sens = _collide(pulled, rho, ux, uy, uz, fluid)
+            layers, sens = _collide(pulled, rho, ux, uy, uz, fluid, with_rho=(s == 0))
             for i in range(19):
                 dst[i, rs, :] = layers[i]
             if s == 0:
                 sens_ref[rs, :] = sens
             else:
-                sens_ref[rs, :] = sens_ref[rs, :] + sens
+                sens2_ref[rs, :] = sens
 
     def indicator(a, off):
         n = sizes[a]
@@ -363,14 +367,15 @@
         vel = velocity.reshape(2, 3, rows, cz)
         mask = pore_mask.reshape(rows, cz)
         vspec = pl.BlockSpec(memory_space=pltpu.VMEM)
-        out, sens = pl.pallas_call(
+        part, sens1, sens2 = pl.pallas_call(
             functools.partial(_kernel, (nx, ny, nz)),
             out_shape=(
                 jax.ShapeDtypeStruct((npop, rows, cz), jnp.float32),
                 jax.ShapeDtypeStruct((rows, cz), jnp.float32),
+                jax.ShapeDtypeStruct((rows, cz), jnp.float32),
             ),
             in_specs=[pl.BlockSpec(memory_space=pltpu.HBM)] * 4,
-            out_specs=(vspec, vspec),
+            out_specs=(vspec, vspec, vspec),
             scratch_shapes=[
                 pltpu.VMEM((npop, rows, cz), jnp.float32),
                 pltpu.VMEM((2, rows, cz), jnp.float32),
@@ -392,7 +397,11 @@
                 collective_id=0, has_side_effects=True, vmem_limit_bytes=67043328
             ),
         )(adj, rho, vel, mask)
-        return out.reshape(npop, cx, cy, cz), sens.reshape(cx, cy, cz)
+        part = part.reshape(npop, cx, cy, cz)
+        speed_x = jnp.array([c[0] for c in VELOCITIES], jnp.float32).reshape(npop, 1, 1, 1)
+        drive = (speed_x - velocity[0, 0][None]) / density[0][None]
+        out = jnp.where(pore_mask[None] > 0, part + drive, part)
+        return out, (sens1 + sens2).reshape(cx, cy, cz)
 
     placed = (
         P(None, "gx", "gy", "gz"),

time: 26.7 us -> 30.4 us (1.14)
  other arithmetic: 0 us -> 4.94 us
  local copies, waits for them, and re-layouts: 3.11 us -> 1.69 us
    unnamed x4 -> x0, local copies, waits for them, and re-layouts: 3.11 us -> none
    select_n x0 -> x1, other arithmetic: none -> 2.58 us  [shards(): out = jnp.where(pore_mask[None] > 0, part + drive, part)]
    add x0 -> x1, other arithmetic: none -> 1.51 us  [shards(): return (out, (sens1 + sens2).reshape(cx, cy, cz))]
    gt x0 -> x1, other arithmetic: none -> 0.85 us  [shards(): out = jnp.where(pore_mask[None] > 0, part + drive, part)]
    div x0 -> x1, local copies, waits for them, and re-layouts: none -> 0.84 us  [shards(): drive = (speed_x - velocity[0, 0][None]) / density[0][None]]
    sub x0 -> x1, local copies, waits for them, and re-layouts: none -> 0.84 us  [shards(): drive = (speed_x - velocity[0, 0][None]) / density[0][None]]
where the time goes in v3:
time: 30.4 us; the launch traced here: 30.1 us
  Pallas kernels  22.8 us (75%)
  other arithmetic  4.94 us (16%)
  local copies, waits for them, and re-layouts  1.69 us (6%)
  between operations  0.64 us (2%)
    pallas_call x1, Pallas kernels, shards(): pl.pallas_call(functools.partial(_kernel, (nx, ny, nz)), out_shape=(jax.S...  22.8 us
    select_n x1, other arithmetic, shards(): out = jnp.where(pore_mask[None] > 0, part + drive, part)  2.58 us
    add x1, other arithmetic, shards(): return (out, (sens1 + sens2).reshape(cx, cy, cz))  1.51 us
    gt x1, other arithmetic, shards(): out = jnp.where(pore_mask[None] > 0, part + drive, part)  0.85 us
    div x1, local copies, waits for them, and re-layouts, shards(): drive = (speed_x - velocity[0, 0][None]) / density[0][None]  0.84 us
    sub x1, local copies, waits for them, and re-layouts, shards(): drive = (speed_x - velocity[0, 0][None]) / density[0][None]  0.84 us

profile of v3, /device:TPU:24, one launch (start us, length us, event | category | flops | bytes accessed | tf_op | source)
XLA Modules:
  0.0 30.1 jit_solution(17762432855964639013)
XLA Ops:
  0.6 22.8 %shard_map.68 = (f32[19,128,128]{2,1,0:T(8,128)}, f32[128,128]{1,0:T(8,128)}, f32[128,128]{1,0:T(8,128)}) custom-call(f32[19,128,128]{2,1,0:T(8,128)} %bitcast.10, f32[2,128,128]{2,1,0:T(8,128)} %bitcast.13, f32[2,3,128,128]{3,2,1,0:T(8,128)} %bitcast.12, s32[128,128]{1,0:T(8,128)} %bitcast.14), custom_call_target="tpu_custom_call" | custom-call | tf_op jit(solution)/shard_map/pallas_call | solution.py:370
  23.5 1.5 %add.7 = f32[128,128]{1,0:T(8,128)} add(f32[128,128]{1,0:T(8,128)} %get-tuple-element.6, f32[128,128]{1,0:T(8,128)} %get-tuple-element.7) | non-fusion elementwise | flops 16384 | bytes 196608 | tf_op jit(solution)/shard_map/add | solution.py:404
  25.0 0.8 %slice_bitcast_fusion = f32[8,16,128]{2,1,0:T(8,128)S(1)} fusion(f32[2,8,16,128]{3,2,1,0:T(8,128)} %param.6), kind=kLoop, calls=%fused_computation.1 | loop fusion | bytes 131072 | tf_op jit(solution)/shard_map/div | solution.py:402
  25.8 0.8 %slice_bitcast_fusion.1 = f32[8,16,128]{2,1,0:T(8,128)S(1)} fusion(f32[2,3,8,16,128]{4,3,2,1,0:T(8,128)} %param.7), kind=kLoop, calls=%fused_computation.2 | loop fusion | bytes 131072 | tf_op jit(solution)/shard_map/sub | solution.py:402
  26.7 0.8 %broadcast_compare_fusion = pred[8,16,128]{2,1,0:T(8,128)(4,1)S(1)} fusion(s32[8,16,128]{2,1,0:T(8,128)} %param.8), kind=kLoop, calls=%fused_computation.3 | loop fusion | flops 16384 | bytes 81920 | tf_op jit(solution)/shard_map/gt | solution.py:403
  27.5 2.6 %add_select_fusion = f32[19,8,16,128]{3,2,1,0:T(8,128)} fusion(f32[19,8,16,128]{3,2,1,0:T(8,128)} %bitcast.11, f32[8,16,128]{2,1,0:T(8,128)S(1)} %slice_bitcast_fusion, f32[8,16,128]{2,1,0:T(8,128)S(1)} %slice_bitcast_fusion.1, f32[19]{0:T(128)} %constant.4.clone, pred[8,16,128]{2,1,0:T(8,128)(4,1)S(1)} %broadcast_compare_fusion), kind=kLoop, calls=%fused_computation | loop fusion | flops 1245184 | bytes 2637900 | tf_op jit(solution)/shard_map/jit(_where)/select_n | solution.py:403

commit v4 on v2

--- a/solution.py
+++ b/solution.py
@@ -350,6 +350,54 @@
     step(1, mid, out_ref, 0)
 
 
+def _writer(chunks, part_hbm, sens_hbm, out_hbm, sens_out, buf, sbuf, sems):
+    npop = part_hbm.shape[0]
+    step = -(-npop // chunks)
+    spans = [(k, min(k + step, npop)) for k in range(0, npop, step)]
+    ins = [
+        pltpu.make_async_copy(part_hbm.at[pl.ds(a, b - a)], buf.at[pl.ds(a, b - a)], sems.at[0, j])
+        for j, (a, b) in enumerate(spans)
+    ]
+    outs = [
+        pltpu.make_async_copy(buf.at[pl.ds(a, b - a)], out_hbm.at[pl.ds(a, b - a)], sems.at[1, j])
+        for j, (a, b) in enumerate(spans)
+    ]
+    sin = pltpu.make_async_copy(sens_hbm, sbuf, sems.at[0, len(spans)])
+    sout = pltpu.make_async_copy(sbuf, sens_out, sems.at[1, len(spans)])
+    sin.start()
+    for copy in ins:
+        copy.start()
+    sin.wait()
+    sout.start()
+    for cin, cout in zip(ins, outs):
+        cin.wait()
+        cout.start()
+    sout.wait()
+    for copy in outs:
+        copy.wait()
+
+
+def _write_out(part, sens, chunks=4):
+    npop, rows, cz = part.shape
+    nspan = len(range(0, npop, -(-npop // chunks)))
+    hbm = pl.BlockSpec(memory_space=pltpu.HBM)
+    return pl.pallas_call(
+        functools.partial(_writer, chunks),
+        out_shape=(
+            jax.ShapeDtypeStruct(part.shape, jnp.float32),
+            jax.ShapeDtypeStruct(sens.shape, jnp.float32),
+        ),
+        in_specs=[hbm, hbm],
+        out_specs=(hbm, hbm),
+        scratch_shapes=[
+            pltpu.VMEM(part.shape, jnp.float32),
+            pltpu.VMEM(sens.shape, jnp.float32),
+            pltpu.SemaphoreType.DMA((2, nspan + 1)),
+        ],
+        compiler_params=pltpu.CompilerParams(vmem_limit_bytes=67043328),
+    )(part, sens)
+
+
 def solution(mesh):
     nx, ny, nz = mesh.shape["gx"], mesh.shape["gy"], mesh.shape["gz"]
     nmsg = len(_messages(8, 16))
@@ -392,6 +440,7 @@
                 collective_id=0, has_side_effects=True, vmem_limit_bytes=67043328
             ),
         )(adj, rho, vel, mask)
+        out, sens = _write_out(out, sens)
         return out.reshape(npop, cx, cy, cz), sens.reshape(cx, cy, cz)
 
     placed = (

time: 26.7 us -> 25.7 us (0.963)
  local copies, waits for them, and re-layouts: 3.11 us -> 0 us
  Pallas kernels: 22.8 us -> 25 us
    unnamed x4 -> x0, local copies, waits for them, and re-layouts: 3.11 us -> none
    pallas_call x0 -> x1, Pallas kernels: none -> 2.12 us  [_write_out(): pl.pallas_call(functools.partial(_writer, chunks), out_shape=(jax.ShapeDt...]
where the time goes in v4:
time: 25.7 us; the launch traced here: 25.6 us
  Pallas kernels  25 us (97%)
  between operations  0.64 us (2%)
    pallas_call x1, Pallas kernels, shards(): pl.pallas_call(functools.partial(_kernel, (nx, ny, nz)), out_shape=(jax.S...  22.8 us
    pallas_call x1, Pallas kernels, _write_out(): pl.pallas_call(functools.partial(_writer, chunks), out_shape=(jax.ShapeDt...  2.12 us

profile of v4, /device:TPU:24, one launch (start us, length us, event | category | flops | bytes accessed | tf_op | source)
XLA Modules:
  0.0 25.6 jit_solution(14075560353139695042)
XLA Ops:
  0.6 22.8 %shard_map.59 = (f32[19,128,128]{2,1,0:T(8,128)}, f32[128,128]{1,0:T(8,128)}) custom-call(f32[19,128,128]{2,1,0:T(8,128)} %bitcast.6, f32[2,128,128]{2,1,0:T(8,128)} %bitcast.8, f32[2,3,128,128]{3,2,1,0:T(8,128)} %bitcast.7, s32[128,128]{1,0:T(8,128)} %bitcast.9), custom_call_target="tpu_custom_call" | custom-call | tf_op jit(solution)/shard_map/pallas_call | solution.py:414
  23.5 2.1 %shard_map.60 = (f32[19,128,128]{2,1,0:T(8,128)}, f32[128,128]{1,0:T(8,128)}) custom-call(f32[19,128,128]{2,1,0:T(8,128)} %get-tuple-element.6.part_hbm, f32[128,128]{1,0:T(8,128)} %get-tuple-element.7.sens_hbm), custom_call_target="tpu_custom_call" | custom-call | tf_op jit(solution)/shard_map/pallas_call | solution.py:384

commit v5 on v4

--- a/solution.py
+++ b/solution.py
@@ -155,7 +155,7 @@
 
 def _kernel(dims, adj_hbm, rho_hbm, vel_hbm, mask_hbm, out_ref, sens_ref,
             adj_ref, rho_ref, vel_ref, mask_ref, load_sem,
-            mid, xh, yh, exy, sy, nt, mh, mt, send_sem, recv_sem):
+            mid, fin, sfin, out_sem, xh, yh, exy, sy, nt, mh, mt, send_sem, recv_sem):
     nx, ny, nz = dims
     cx, cy, cz = 8, 16, 128
     rows = cx * cy
@@ -305,8 +305,14 @@
             out.append(plane)
         return out
 
+    def flush(p):
+        rs = pl.ds(p * cy, cy)
+        pltpu.make_async_copy(fin.at[:, rs, :], out_ref.at[:, rs, :], out_sem.at[p]).start()
+
     def step(s, src, dst, level):
         for p in range(cx):
+            if s == 1 and p >= 1:
+                flush(p - 1)
             rs = pl.ds(p * cy, cy)
             pulled = pulled_plane(s, src, p)
             rho = rho_ref[level, rs, :]
@@ -318,9 +324,9 @@
             for i in range(19):
                 dst[i, rs, :] = layers[i]
             if s == 0:
-                sens_ref[rs, :] = sens
+                sfin[rs, :] = sens
             else:
-                sens_ref[rs, :] = sens_ref[rs, :] + sens
+                sfin[rs, :] = sfin[rs, :] + sens
 
     def indicator(a, off):
         n = sizes[a]
@@ -347,7 +353,14 @@
     prepare(1, mid)
     send(1, mid)
     finish(1, mid)
-    step(1, mid, out_ref, 0)
+    step(1, mid, fin, 0)
+    flush(cx - 1)
+    sens_copy = pltpu.make_async_copy(sfin, sens_ref, out_sem.at[cx])
+    sens_copy.start()
+    for p in range(cx):
+        rs = pl.ds(p * cy, cy)
+        pltpu.make_async_copy(fin.at[:, rs, :], out_ref.at[:, rs, :], out_sem.at[p]).wait()
+    sens_copy.wait()
 
 
 def _writer(chunks, part_hbm, sens_hbm, out_hbm, sens_out, buf, sbuf, sems):
@@ -377,7 +390,7 @@
         copy.wait()
 
 
-def _write_out(part, sens, chunks=4):
+def _write_out(part, sens, chunks=8):
     npop, rows, cz = part.shape
     nspan = len(range(0, npop, -(-npop // chunks)))
     hbm = pl.BlockSpec(memory_space=pltpu.HBM)
@@ -418,7 +431,7 @@
                 jax.ShapeDtypeStruct((rows, cz), jnp.float32),
             ),
             in_specs=[pl.BlockSpec(memory_space=pltpu.HBM)] * 4,
-            out_specs=(vspec, vspec),
+            out_specs=(pl.BlockSpec(memory_space=pltpu.HBM), pl.BlockSpec(memory_space=pltpu.HBM)),
             scratch_shapes=[
                 pltpu.VMEM((npop, rows, cz), jnp.float32),
                 pltpu.VMEM((2, rows, cz), jnp.float32),
@@ -426,6 +439,9 @@
                 pltpu.VMEM((rows, cz), jnp.int32),
                 pltpu.SemaphoreType.DMA((4,)),
                 pltpu.VMEM((npop, rows, cz), jnp.float32),
+                pltpu.VMEM((npop, rows, cz), jnp.float32),
+                pltpu.VMEM((rows, cz), jnp.float32),
+                pltpu.SemaphoreType.DMA((cx + 1,)),
                 pltpu.VMEM((2, 2, 5, cy, cz), jnp.float32),
                 pltpu.VMEM((2, 2, 5, cx, cz), jnp.float32),
                 pltpu.VMEM((2, 4, 8, cz), jnp.float32),

time: 25.7 us -> 25.5 us (level)
    pallas_call x1, Pallas kernels: 22.8 us -> 22.5 us  [shards(): pl.pallas_call(functools.partial(_kernel, (nx, ny, nz)), out_shape=(jax.S...]
where the time goes in v5:
time: 25.5 us; the launch traced here: 25.4 us
  Pallas kernels  24.8 us (97%)
  between operations  0.64 us (3%)
    pallas_call x1, Pallas kernels, shards(): pl.pallas_call(functools.partial(_kernel, (nx, ny, nz)), out_shape=(jax.S...  22.5 us
    pallas_call x1, Pallas kernels, _write_out(): pl.pallas_call(functools.partial(_writer, chunks), out_shape=(jax.ShapeDt...  2.21 us

profile of v5, /device:TPU:24, one launch (start us, length us, event | category | flops | bytes accessed | tf_op | source)
XLA Modules:
  0.0 25.4 jit_solution(8508295770238483408)
XLA Ops:
  0.6 22.5 %shard_map.59 = (f32[19,128,128]{2,1,0:T(8,128)}, f32[128,128]{1,0:T(8,128)}) custom-call(f32[19,128,128]{2,1,0:T(8,128)} %bitcast.6, f32[2,128,128]{2,1,0:T(8,128)} %bitcast.8, f32[2,3,128,128]{3,2,1,0:T(8,128)} %bitcast.7, s32[128,128]{1,0:T(8,128)} %bitcast.9), custom_call_target="tpu_custom_call" | custom-call | tf_op jit(solution)/shard_map/pallas_call | solution.py:427
  23.2 2.2 %shard_map.60 = (f32[19,128,128]{2,1,0:T(8,128)}, f32[128,128]{1,0:T(8,128)}) custom-call(f32[19,128,128]{2,1,0:T(8,128)} %get-tuple-element.6.part_hbm, f32[128,128]{1,0:T(8,128)} %get-tuple-element.7.sens_hbm), custom_call_target="tpu_custom_call" | custom-call | tf_op jit(solution)/shard_map/pallas_call | solution.py:397

commit v6 on v5

--- a/solution.py
+++ b/solution.py
@@ -47,12 +47,12 @@
 def _messages(cx, cy):
     rows = cx * cy
     msgs = []
-    for k, pop in enumerate(CXP):
-        msgs.append(((-1, 0, 0), ("S", pop, 0, cy), ("XH", 1, k)))
-    for k, pop in enumerate(CXM):
-        msgs.append(((1, 0, 0), ("S", pop, rows - cy, cy), ("XH", 0, k)))
     msgs.append(((0, -1, 0), ("SY", 0), ("YH", 1)))
     msgs.append(((0, 1, 0), ("SY", 1), ("YH", 0)))
+    msgs.append(((0, -1, -1), ("NT", 24, 8), ("MH", 1, 56, 8)))
+    msgs.append(((0, 1, -1), ("NT", 32, 8), ("MH", 1, 64, 8)))
+    msgs.append(((0, 1, 1), ("NT", 64, 8), ("MH", 0, 56, 8)))
+    msgs.append(((0, -1, 1), ("NT", 72, 8), ("MH", 0, 64, 8)))
     msgs.append(((-1, -1, 0), ("S", 7, 0, 8), ("EXY", 0)))
     msgs.append(((1, 1, 0), ("S", 8, rows - 8, 8), ("EXY", 1)))
     msgs.append(((-1, 1, 0), ("S", 9, cy - 8, 8), ("EXY", 2)))
@@ -63,10 +63,8 @@
     msgs.append(((1, 0, -1), ("NT", 16, 8), ("MH", 1, 48, 8)))
     msgs.append(((1, 0, 1), ("NT", 48, 8), ("MH", 0, 40, 8)))
     msgs.append(((-1, 0, 1), ("NT", 56, 8), ("MH", 0, 48, 8)))
-    msgs.append(((0, -1, -1), ("NT", 24, 8), ("MH", 1, 56, 8)))
-    msgs.append(((0, 1, -1), ("NT", 32, 8), ("MH", 1, 64, 8)))
-    msgs.append(((0, 1, 1), ("NT", 64, 8), ("MH", 0, 56, 8)))
-    msgs.append(((0, -1, 1), ("NT", 72, 8), ("MH", 0, 64, 8)))
+    msgs.append(((-1, 0, 0), ("SX", 0), ("XH", 1)))
+    msgs.append(((1, 0, 0), ("SX", 1), ("XH", 0)))
     return msgs
 
 
@@ -155,7 +153,7 @@
 
 def _kernel(dims, adj_hbm, rho_hbm, vel_hbm, mask_hbm, out_ref, sens_ref,
             adj_ref, rho_ref, vel_ref, mask_ref, load_sem,
-            mid, fin, sfin, out_sem, xh, yh, exy, sy, nt, mh, mt, send_sem, recv_sem):
+            mid, fin, sfin, out_sem, xh, yh, exy, sy, sx, nt, mh, mt, send_sem, recv_sem):
     nx, ny, nz = dims
     cx, cy, cz = 8, 16, 128
     rows = cx * cy
@@ -203,6 +201,9 @@
     msgs = _messages(cx, cy)
 
     def prepare(s, src):
+        for side, pops, q in ((0, CXP, 0), (1, CXM, cx - 1)):
+            for k, pop in enumerate(pops):
+                sx[s, side, k] = src[pop, pl.ds(q * cy, cy), :]
         for side, pops, y in ((0, CYP, 0), (1, CYM, cy - 1)):
             for k, pop in enumerate(pops):
                 sy[s, side, k] = src[pop, pl.ds(y, cx, stride=cy), :]
@@ -218,10 +219,12 @@
             sref = src.at[so[1], pl.ds(so[2] % rows, so[3]), :]
         elif so[0] == "SY":
             sref = sy.at[s, so[1]]
+        elif so[0] == "SX":
+            sref = sx.at[s, so[1]]
         else:
             sref = nt.at[s, pl.ds(so[1], so[2]), :]
         if de[0] == "XH":
-            dref = xh.at[s, de[1], de[2]]
+            dref = xh.at[s, de[1]]
         elif de[0] == "YH":
             dref = yh.at[s, de[1]]
         elif de[0] == "EXY":
@@ -446,6 +449,7 @@
                 pltpu.VMEM((2, 2, 5, cx, cz), jnp.float32),
                 pltpu.VMEM((2, 4, 8, cz), jnp.float32),
                 pltpu.VMEM((2, 2, 5, cx, cz), jnp.float32),
+                pltpu.VMEM((2, 2, 5, cy, cz), jnp.float32),
                 pltpu.VMEM((2, rows, cz), jnp.float32),
                 pltpu.VMEM((2, 2, rows, cz), jnp.float32),
                 pltpu.VMEM((2, 2, rows, cz), jnp.float32),

time: 25.5 us -> 25.1 us (0.984)
  Pallas kernels: 24.8 us -> 24.3 us
    pallas_call x1, Pallas kernels: 22.5 us -> 22.1 us  [shards(): pl.pallas_call(functools.partial(_kernel, (nx, ny, nz)), out_shape=(jax.S...]
where the time goes in v6:
time: 25.1 us; the launch traced here: 24.9 us
  Pallas kernels  24.3 us (97%)
  between operations  0.64 us (3%)
    pallas_call x1, Pallas kernels, shards(): pl.pallas_call(functools.partial(_kernel, (nx, ny, nz)), out_shape=(jax.S...  22.1 us
    pallas_call x1, Pallas kernels, _write_out(): pl.pallas_call(functools.partial(_writer, chunks), out_shape=(jax.ShapeDt...  2.21 us

profile of v6, /device:TPU:24, one launch (start us, length us, event | category | flops | bytes accessed | tf_op | source)
XLA Modules:
  0.0 24.9 jit_solution(17794217705536278232)
XLA Ops:
  0.6 22.1 %shard_map.59 = (f32[19,128,128]{2,1,0:T(8,128)}, f32[128,128]{1,0:T(8,128)}) custom-call(f32[19,128,128]{2,1,0:T(8,128)} %bitcast.6, f32[2,128,128]{2,1,0:T(8,128)} %bitcast.8, f32[2,3,128,128]{3,2,1,0:T(8,128)} %bitcast.7, s32[128,128]{1,0:T(8,128)} %bitcast.9), custom_call_target="tpu_custom_call" | custom-call | tf_op jit(solution)/shard_map/pallas_call | solution.py:430
  22.7 2.2 %shard_map.60 = (f32[19,128,128]{2,1,0:T(8,128)}, f32[128,128]{1,0:T(8,128)}) custom-call(f32[19,128,128]{2,1,0:T(8,128)} %get-tuple-element.6.part_hbm, f32[128,128]{1,0:T(8,128)} %get-tuple-element.7.sens_hbm), custom_call_target="tpu_custom_call" | custom-call | tf_op jit(solution)/shard_map/pallas_call | solution.py:400

commit v7 on v6

--- a/solution.py
+++ b/solution.py
@@ -366,30 +366,18 @@
     sens_copy.wait()
 
 
-def _writer(chunks, part_hbm, sens_hbm, out_hbm, sens_out, buf, sbuf, sems):
+def _writer(chunks, part_hbm, sens_hbm, out_hbm, sens_out, sems):
     npop = part_hbm.shape[0]
     step = -(-npop // chunks)
     spans = [(k, min(k + step, npop)) for k in range(0, npop, step)]
-    ins = [
-        pltpu.make_async_copy(part_hbm.at[pl.ds(a, b - a)], buf.at[pl.ds(a, b - a)], sems.at[0, j])
+    copies = [
+        pltpu.make_async_copy(part_hbm.at[pl.ds(a, b - a)], out_hbm.at[pl.ds(a, b - a)], sems.at[j])
         for j, (a, b) in enumerate(spans)
     ]
-    outs = [
-        pltpu.make_async_copy(buf.at[pl.ds(a, b - a)], out_hbm.at[pl.ds(a, b - a)], sems.at[1, j])
-        for j, (a, b) in enumerate(spans)
-    ]
-    sin = pltpu.make_async_copy(sens_hbm, sbuf, sems.at[0, len(spans)])
-    sout = pltpu.make_async_copy(sbuf, sens_out, sems.at[1, len(spans)])
-    sin.start()
-    for copy in ins:
+    copies.append(pltpu.make_async_copy(sens_hbm, sens_out, sems.at[len(spans)]))
+    for copy in copies:
         copy.start()
-    sin.wait()
-    sout.start()
-    for cin, cout in zip(ins, outs):
-        cin.wait()
-        cout.start()
-    sout.wait()
-    for copy in outs:
+    for copy in copies:
         copy.wait()
 
 
@@ -405,11 +393,7 @@
         ),
         in_specs=[hbm, hbm],
         out_specs=(hbm, hbm),
-        scratch_shapes=[
-            pltpu.VMEM(part.shape, jnp.float32),
-            pltpu.VMEM(sens.shape, jnp.float32),
-            pltpu.SemaphoreType.DMA((2, nspan + 1)),
-        ],
+        scratch_shapes=[pltpu.SemaphoreType.DMA((nspan + 1,))],
         compiler_params=pltpu.CompilerParams(vmem_limit_bytes=67043328),
     )(part, sens)
 

time: 25.1 us -> 63.7 us (2.54)
  Pallas kernels: 24.3 us -> 63 us
    pallas_call x1, Pallas kernels: 2.21 us -> 40.9 us  [_write_out(): pl.pallas_call(functools.partial(_writer, chunks), out_shape=(jax.ShapeDt...]
where the time goes in v7:
time: 63.7 us; the launch traced here: 63.6 us
  Pallas kernels  63 us (99%)
  between operations  0.64 us (1%)
    pallas_call x1, Pallas kernels, _write_out(): pl.pallas_call(functools.partial(_writer, chunks), out_shape=(jax.ShapeDt...  40.9 us
    pallas_call x1, Pallas kernels, shards(): pl.pallas_call(functools.partial(_kernel, (nx, ny, nz)), out_shape=(jax.S...  22.1 us

profile of v7, /device:TPU:24, one launch (start us, length us, event | category | flops | bytes accessed | tf_op | source)
XLA Modules:
  0.0 63.6 jit_solution(16315386139882011701)
XLA Ops:
  0.6 22.1 %shard_map.59 = (f32[19,128,128]{2,1,0:T(8,128)}, f32[128,128]{1,0:T(8,128)}) custom-call(f32[19,128,128]{2,1,0:T(8,128)} %bitcast.6, f32[2,128,128]{2,1,0:T(8,128)} %bitcast.8, f32[2,3,128,128]{3,2,1,0:T(8,128)} %bitcast.7, s32[128,128]{1,0:T(8,128)} %bitcast.9), custom_call_target="tpu_custom_call" | custom-call | tf_op jit(solution)/shard_map/pallas_call | solution.py:414
  22.7 40.9 %shard_map.60 = (f32[19,128,128]{2,1,0:T(8,128)}, f32[128,128]{1,0:T(8,128)}) custom-call(f32[19,128,128]{2,1,0:T(8,128)} %get-tuple-element.6.part_hbm, f32[128,128]{1,0:T(8,128)} %get-tuple-element.7.sens_hbm), custom_call_target="tpu_custom_call" | custom-call | tf_op jit(solution)/shard_map/pallas_call | solution.py:388

commit v8 on v1

--- a/solution.py
+++ b/solution.py
@@ -47,12 +47,12 @@
 def _messages(cx, cy):
     rows = cx * cy
     msgs = []
-    for k, pop in enumerate(CXP):
-        msgs.append(((-1, 0, 0), ("S", pop, 0, cy), ("XH", 1, k)))
-    for k, pop in enumerate(CXM):
-        msgs.append(((1, 0, 0), ("S", pop, rows - cy, cy), ("XH", 0, k)))
     msgs.append(((0, -1, 0), ("SY", 0), ("YH", 1)))
     msgs.append(((0, 1, 0), ("SY", 1), ("YH", 0)))
+    msgs.append(((0, -1, -1), ("NT", 24, 8), ("MH", 1, 56, 8)))
+    msgs.append(((0, 1, -1), ("NT", 32, 8), ("MH", 1, 64, 8)))
+    msgs.append(((0, 1, 1), ("NT", 64, 8), ("MH", 0, 56, 8)))
+    msgs.append(((0, -1, 1), ("NT", 72, 8), ("MH", 0, 64, 8)))
     msgs.append(((-1, -1, 0), ("S", 7, 0, 8), ("EXY", 0)))
     msgs.append(((1, 1, 0), ("S", 8, rows - 8, 8), ("EXY", 1)))
     msgs.append(((-1, 1, 0), ("S", 9, cy - 8, 8), ("EXY", 2)))
@@ -63,10 +63,8 @@
     msgs.append(((1, 0, -1), ("NT", 16, 8), ("MH", 1, 48, 8)))
     msgs.append(((1, 0, 1), ("NT", 48, 8), ("MH", 0, 40, 8)))
     msgs.append(((-1, 0, 1), ("NT", 56, 8), ("MH", 0, 48, 8)))
-    msgs.append(((0, -1, -1), ("NT", 24, 8), ("MH", 1, 56, 8)))
-    msgs.append(((0, 1, -1), ("NT", 32, 8), ("MH", 1, 64, 8)))
-    msgs.append(((0, 1, 1), ("NT", 64, 8), ("MH", 0, 56, 8)))
-    msgs.append(((0, -1, 1), ("NT", 72, 8), ("MH", 0, 64, 8)))
+    msgs.append(((-1, 0, 0), ("SX", 0), ("XH", 1)))
+    msgs.append(((1, 0, 0), ("SX", 1), ("XH", 0)))
     return msgs
 
 
@@ -153,13 +151,8 @@
     return layers, sens
 
 
-def _kernel(dims, adj_ref, rho_ref, vel_ref, mask_ref, out_ref, sens_ref,
-            mid, xh, yh, exy, sy, nt, mh, mt, send_sem, recv_sem):
-    nx, ny, nz = dims
-    cx, cy, cz = 8, 16, 128
-    rows = cx * cy
+def _where(dims):
     me = (lax.axis_index("gx"), lax.axis_index("gy"), lax.axis_index("gz"))
-    sizes = (nx, ny, nz)
 
     def exists(d):
         cond = None
@@ -167,85 +160,39 @@
             if d[a] == 0:
                 continue
             v = me[a] + d[a]
-            c = (v >= 0) if d[a] < 0 else (v < sizes[a])
+            c = (v >= 0) if d[a] < 0 else (v < dims[a])
             cond = c if cond is None else jnp.logical_and(cond, c)
         return cond
 
     def target(d):
         return tuple(me[a] + d[a] for a in range(3))
 
-    xh[...] = jnp.zeros(xh.shape, jnp.float32)
-    yh[...] = jnp.zeros(yh.shape, jnp.float32)
-    exy[...] = jnp.zeros(exy.shape, jnp.float32)
-    mh[...] = jnp.zeros(mh.shape, jnp.float32)
-
-    barrier = pltpu.get_barrier_semaphore()
-    for d in NEIGHBOURS:
-        @pl.when(exists(d))
+    return me, exists, target
+
+
+def _zero_missing(exists, xh, yh, exy, mh):
+    for d, so, de in _messages(8, 16):
+        back = tuple(-v for v in d)
+
+        @pl.when(jnp.logical_not(exists(back)))
         def _():
-            pl.semaphore_signal(barrier, inc=1, device_id=target(d), device_id_type=MESH)
-
+            if de[0] == "XH":
+                xh[de[1]] = jnp.zeros(xh.shape[1:], jnp.float32)
+            elif de[0] == "YH":
+                yh[de[1]] = jnp.zeros(yh.shape[1:], jnp.float32)
+            elif de[0] == "EXY":
+                exy[de[1]] = jnp.zeros(exy.shape[1:], jnp.float32)
+            else:
+                mh[de[1], pl.ds(de[2], de[3]), :] = jnp.zeros((de[3], mh.shape[-1]), jnp.float32)
+
+
+def _step(s, src, xh, yh, exy, mt, rho_ref, vel_ref, mask_ref, level, emit, before=None):
+    cx, cy, cz = 8, 16, 128
     lane = lax.broadcasted_iota(jnp.int32, (cy, cz), 1)
     lane1 = lax.broadcasted_iota(jnp.int32, (1, cz), 1)
     row = lax.broadcasted_iota(jnp.int32, (cy, cz), 0)
-    lane_big = lax.broadcasted_iota(jnp.int32, (rows, cz), 1)
-
-    msgs = _messages(cx, cy)
-
-    def prepare(s, src):
-        for side, pops, y in ((0, CYP, 0), (1, CYM, cy - 1)):
-            for k, pop in enumerate(pops):
-                sy[s, side, k] = src[pop, pl.ds(y, cx, stride=cy), :]
-        n = jnp.zeros((rows, cz), jnp.float32)
-        for j, (pop, z) in enumerate(ZCOLS):
-            zz = z % cz
-            n = jnp.where(lane_big == 8 * j, pltpu.roll(src[pop], (8 * j - zz) % cz, 1), n)
-        nt[s] = n.T
-
-    def descriptor(s, src, m, t):
-        d, so, de = msgs[t]
-        if so[0] == "S":
-            sref = src.at[so[1], pl.ds(so[2] % rows, so[3]), :]
-        elif so[0] == "SY":
-            sref = sy.at[s, so[1]]
-        else:
-            sref = nt.at[s, pl.ds(so[1], so[2]), :]
-        if de[0] == "XH":
-            dref = xh.at[s, de[1], de[2]]
-        elif de[0] == "YH":
-            dref = yh.at[s, de[1]]
-        elif de[0] == "EXY":
-            dref = exy.at[s, de[1]]
-        else:
-            dref = mh.at[s, de[1], pl.ds(de[2], de[3]), :]
-        return pltpu.make_async_remote_copy(
-            src_ref=sref, dst_ref=dref, send_sem=send_sem.at[s, t], recv_sem=recv_sem.at[s, t],
-            device_id=target(d), device_id_type=MESH)
-
-    def send(s, src):
-        for t in range(len(msgs)):
-            d = msgs[t][0]
-
-            @pl.when(exists(d))
-            def _():
-                descriptor(s, src, msgs, t).start()
-
-    def finish(s, src):
-        for t in range(len(msgs)):
-            d = msgs[t][0]
-            back = tuple(-v for v in d)
-
-            @pl.when(exists(back))
-            def _():
-                descriptor(s, src, msgs, t).wait_recv()
-
-            @pl.when(exists(d))
-            def _():
-                descriptor(s, src, msgs, t).wait_send()
-        for side in range(2):
-            mt[s, side] = mh[s, side].T
-
-    def pulled_plane(s, src, p):
+
+    def pulled_plane(p):
         out = []
         for i in range(19):
             vx, vy, vz = VELOCITIES[i]
@@ -263,7 +210,7 @@
                     col = ZFACE_COL[i]
                 else:
                     col, r0 = XZ_EDGE[i]
-                    zc = mt[s, side, pl.ds(r0 % rows, cy), :]
+                    zc = mt[s, side, pl.ds(r0 % (cx * cy), cy), :]
                 if vz > 0:
                     plane = jnp.where(lane == cz - 1, pltpu.roll(zc, (cz - 1 - col) % cz, 1),
                                       pltpu.roll(plane, cz - 1, 1))
@@ -295,50 +242,194 @@
             out.append(plane)
         return out
 
-    def step(s, src, dst, level):
-        for p in range(cx):
-            rs = pl.ds(p * cy, cy)
-            pulled = pulled_plane(s, src, p)
-            rho = rho_ref[level, rs, :]
-            ux = vel_ref[level, 0, rs, :]
-            uy = vel_ref[level, 1, rs, :]
-            uz = vel_ref[level, 2, rs, :]
-            fluid = mask_ref[rs, :] > 0
-            layers, sens = _collide(pulled, rho, ux, uy, uz, fluid)
-            for i in range(19):
-                dst[i, rs, :] = layers[i]
-            if s == 0:
-                sens_ref[rs, :] = sens
-            else:
-                sens_ref[rs, :] = sens_ref[rs, :] + sens
-
-    def indicator(a, off):
-        n = sizes[a]
-        if off < 0:
-            return (me[a] + n - 1) // n
-        if off > 0:
-            return (2 * n - 2 - me[a]) // n
-        return 1
+    for p in range(cx):
+        if before is not None:
+            before(p)
+        rs = pl.ds(p * cy, cy)
+        pulled = pulled_plane(p)
+        rho = rho_ref[level, rs, :]
+        ux = vel_ref[level, 0, rs, :]
+        uy = vel_ref[level, 1, rs, :]
+        uz = vel_ref[level, 2, rs, :]
+        fluid = mask_ref[rs, :] > 0
+        layers, sens = _collide(pulled, rho, ux, uy, uz, fluid)
+        emit(p, rs, layers, sens)
+
+
+def _kernel(dims, adj_hbm, rho_hbm, vel_hbm, mask_hbm,
+            mid_out, sens_out, xh_out, yh_out, exy_out, mh_out,
+            adj_ref, rho_ref, vel_ref, mask_ref, load_sem,
+            mid, sfin, out_sem, xh, yh, exy, sy, sx, nt, mh, mt, send_sem, recv_sem):
+    cx, cy, cz = 8, 16, 128
+    rows = cx * cy
+    me, exists, target = _where(dims)
+
+    barrier = pltpu.get_barrier_semaphore()
+    for d in NEIGHBOURS:
+        @pl.when(exists(d))
+        def _():
+            pl.semaphore_signal(barrier, inc=1, device_id=target(d), device_id_type=MESH)
+
+    loads = [
+        pltpu.make_async_copy(src, dst, load_sem.at[k])
+        for k, (src, dst) in enumerate(
+            ((adj_hbm, adj_ref), (vel_hbm, vel_ref), (rho_hbm, rho_ref), (mask_hbm, mask_ref))
+        )
+    ]
+    for copy in loads:
+        copy.start()
+
+    mh[0, :, pl.ds(72, rows - 72), :] = jnp.zeros((2, rows - 72, cz), jnp.float32)
+    _zero_missing(exists, xh.at[0], yh.at[0], exy.at[0], mh.at[0])
+
+    lane_big = lax.broadcasted_iota(jnp.int32, (rows, cz), 1)
+    msgs = _messages(cx, cy)
+
+    def prepare(s, src):
+        for side, pops, q in ((0, CXP, 0), (1, CXM, cx - 1)):
+            for k, pop in enumerate(pops):
+                sx[s, side, k] = src[pop, pl.ds(q * cy, cy), :]
+        for side, pops, y in ((0, CYP, 0), (1, CYM, cy - 1)):
+            for k, pop in enumerate(pops):
+                sy[s, side, k] = src[pop, pl.ds(y, cx, stride=cy), :]
+        n = jnp.zeros((rows, cz), jnp.float32)
+        for j, (pop, z) in enumerate(ZCOLS):
+            zz = z % cz
+            n = jnp.where(lane_big == 8 * j, pltpu.roll(src[pop], (8 * j - zz) % cz, 1), n)
+        nt[s] = n.T
+
+    def descriptor(s, src, t):
+        d, so, de = msgs[t]
+        if so[0] == "S":
+            sref = src.at[so[1], pl.ds(so[2] % rows, so[3]), :]
+        elif so[0] == "SY":
+            sref = sy.at[s, so[1]]
+        elif so[0] == "SX":
+            sref = sx.at[s, so[1]]
+        else:
+            sref = nt.at[s, pl.ds(so[1], so[2]), :]
+        bufs = {"XH": (xh.at[0], xh_out), "YH": (yh.at[0], yh_out), "EXY": (exy.at[0], exy_out),
+                "MH": (mh.at[0], mh_out)}[de[0]][s]
+        if de[0] == "MH":
+            dref = bufs.at[de[1], pl.ds(de[2], de[3]), :]
+        else:
+            dref = bufs.at[de[1]]
+        return pltpu.make_async_remote_copy(
+            src_ref=sref, dst_ref=dref, send_sem=send_sem.at[s, t], recv_sem=recv_sem.at[s, t],
+            device_id=target(d), device_id_type=MESH)
+
+    def send(s, src):
+        for t in range(len(msgs)):
+            @pl.when(exists(msgs[t][0]))
+            def _():
+                descriptor(s, src, t).start()
+
+    def finish(s, src):
+        for t in range(len(msgs)):
+            d = msgs[t][0]
+            back = tuple(-v for v in d)
+
+            @pl.when(exists(back))
+            def _():
+                descriptor(s, src, t).wait_recv()
+
+            @pl.when(exists(d))
+            def _():
+                descriptor(s, src, t).wait_send()
 
     peers = 0
     for d in NEIGHBOURS:
         term = 1
         for a in range(3):
-            term = term * indicator(a, d[a])
+            n = dims[a]
+            if d[a] < 0:
+                term = term * ((me[a] + n - 1) // n)
+            elif d[a] > 0:
+                term = term * ((2 * n - 2 - me[a]) // n)
         peers = peers + term
+    loads[0].wait()
     prepare(0, adj_ref)
     pl.semaphore_wait(barrier, peers)
     send(0, adj_ref)
+    for copy in loads[1:]:
+        copy.wait()
     finish(0, adj_ref)
-    step(0, adj_ref, mid, 1)
+    for side in range(2):
+        mt[0, side] = mh[0, side].T
+
+    def flush(p):
+        rs = pl.ds(p * cy, cy)
+        pltpu.make_async_copy(mid.at[:, rs, :], mid_out.at[:, rs, :], out_sem.at[p]).start()
+
+    def emit(p, rs, layers, sens):
+        for i in range(19):
+            mid[i, rs, :] = layers[i]
+        sfin[rs, :] = sens
+
+    _step(0, adj_ref, xh, yh, exy, mt, rho_ref, vel_ref, mask_ref, 1, emit,
+          before=lambda p: flush(p - 1) if p >= 1 else None)
+    flush(cx - 1)
+    sens_copy = pltpu.make_async_copy(sfin, sens_out, out_sem.at[cx])
+    sens_copy.start()
     prepare(1, mid)
     send(1, mid)
     finish(1, mid)
-    step(1, mid, out_ref, 0)
+    for p in range(cx):
+        rs = pl.ds(p * cy, cy)
+        pltpu.make_async_copy(mid.at[:, rs, :], mid_out.at[:, rs, :], out_sem.at[p]).wait()
+    sens_copy.wait()
+
+
+def _last(dims, mid_hbm, s1_hbm, xh_hbm, yh_hbm, exy_hbm, mh_hbm, rho_hbm, vel_hbm, mask_hbm,
+          out_hbm, sens_hbm,
+          mid, s1, xh, yh, exy, mh, mt, rho, vel, mask, fin, sfin, in_sem, out_sem):
+    cx, cy, cz = 8, 16, 128
+    rows = cx * cy
+    me, exists, target = _where(dims)
+    mh[...] = jnp.zeros(mh.shape, jnp.float32)
+    used = 72
+    loads = [
+        pltpu.make_async_copy(xh_hbm, xh.at[0], in_sem.at[0]),
+        pltpu.make_async_copy(yh_hbm, yh.at[0], in_sem.at[1]),
+        pltpu.make_async_copy(exy_hbm, exy.at[0], in_sem.at[2]),
+        pltpu.make_async_copy(mh_hbm.at[:, pl.ds(0, used), :], mh.at[:, pl.ds(0, used), :], in_sem.at[3]),
+        pltpu.make_async_copy(rho_hbm.at[pl.ds(0, 1)], rho, in_sem.at[4]),
+        pltpu.make_async_copy(vel_hbm.at[pl.ds(0, 1)], vel, in_sem.at[5]),
+        pltpu.make_async_copy(mask_hbm, mask, in_sem.at[6]),
+        pltpu.make_async_copy(s1_hbm, s1, in_sem.at[7]),
+        pltpu.make_async_copy(mid_hbm, mid, in_sem.at[8]),
+    ]
+    for copy in loads:
+        copy.start()
+    for copy in loads:
+        copy.wait()
+    _zero_missing(exists, xh.at[0], yh.at[0], exy.at[0], mh)
+
+    for side in range(2):
+        mt[0, side] = mh[side].T
+
+    def flush(p):
+        rs = pl.ds(p * cy, cy)
+        pltpu.make_async_copy(fin.at[:, rs, :], out_hbm.at[:, rs, :], out_sem.at[p]).start()
+
+    def emit(p, rs, layers, sens):
+        for i in range(19):
+            fin[i, rs, :] = layers[i]
+        sfin[rs, :] = s1[rs, :] + sens
+
+    _step(0, mid, xh, yh, exy, mt, rho, vel, mask, 0, emit,
+          before=lambda p: flush(p - 1) if p >= 1 else None)
+    flush(cx - 1)
+    sens_copy = pltpu.make_async_copy(sfin, sens_hbm, out_sem.at[cx])
+    sens_copy.start()
+    for p in range(cx):
+        rs = pl.ds(p * cy, cy)
+        pltpu.make_async_copy(fin.at[:, rs, :], out_hbm.at[:, rs, :], out_sem.at[p]).wait()
+    sens_copy.wait()
 
 
 def solution(mesh):
-    nx, ny, nz = mesh.shape["gx"], mesh.shape["gy"], mesh.shape["gz"]
+    dims = (mesh.shape["gx"], mesh.shape["gy"], mesh.shape["gz"])
     nmsg = len(_messages(8, 16))
 
     def shards(adjoint, density, velocity, pore_mask):
@@ -349,31 +440,72 @@
         rho = density.reshape(2, rows, cz)
         vel = velocity.reshape(2, 3, rows, cz)
         mask = pore_mask.reshape(rows, cz)
-        vspec = pl.BlockSpec(memory_space=pltpu.VMEM)
-        out, sens = pl.pallas_call(
-            functools.partial(_kernel, (nx, ny, nz)),
+        hbm = pl.BlockSpec(memory_space=pltpu.HBM)
+        f32 = jnp.float32
+        halo_shapes = (
+            jax.ShapeDtypeStruct((2, 5, cy, cz), f32),
+            jax.ShapeDtypeStruct((2, 5, cx, cz), f32),
+            jax.ShapeDtypeStruct((4, 8, cz), f32),
+            jax.ShapeDtypeStruct((2, rows, cz), f32),
+        )
+        mid, s1, xh2, yh2, exy2, mh2 = pl.pallas_call(
+            functools.partial(_kernel, dims),
             out_shape=(
-                jax.ShapeDtypeStruct((npop, rows, cz), jnp.float32),
-                jax.ShapeDtypeStruct((rows, cz), jnp.float32),
-            ),
-            in_specs=[vspec] * 4,
-            out_specs=(vspec, vspec),
+                jax.ShapeDtypeStruct((npop, rows, cz), f32),
+                jax.ShapeDtypeStruct((rows, cz), f32),
+            ) + halo_shapes,
+            in_specs=[hbm] * 4,
+            out_specs=(hbm,) * 6,
             scratch_shapes=[
-                pltpu.VMEM((npop, rows, cz), jnp.float32),
-                pltpu.VMEM((2, 2, 5, cy, cz), jnp.float32),
-                pltpu.VMEM((2, 2, 5, cx, cz), jnp.float32),
-                pltpu.VMEM((2, 4, 8, cz), jnp.float32),
-                pltpu.VMEM((2, 2, 5, cx, cz), jnp.float32),
-                pltpu.VMEM((2, rows, cz), jnp.float32),
-                pltpu.VMEM((2, 2, rows, cz), jnp.float32),
-                pltpu.VMEM((2, 2, rows, cz), jnp.float32),
+                pltpu.VMEM((npop, rows, cz), f32),
+                pltpu.VMEM((2, rows, cz), f32),
+                pltpu.VMEM((2, 3, rows, cz), f32),
+                pltpu.VMEM((rows, cz), jnp.int32),
+                pltpu.SemaphoreType.DMA((4,)),
+                pltpu.VMEM((npop, rows, cz), f32),
+                pltpu.VMEM((rows, cz), f32),
+                pltpu.SemaphoreType.DMA((cx + 1,)),
+                pltpu.VMEM((1, 2, 5, cy, cz), f32),
+                pltpu.VMEM((1, 2, 5, cx, cz), f32),
+                pltpu.VMEM((1, 4, 8, cz), f32),
+                pltpu.VMEM((2, 2, 5, cx, cz), f32),
+                pltpu.VMEM((2, 2, 5, cy, cz), f32),
+                pltpu.VMEM((2, rows, cz), f32),
+                pltpu.VMEM((1, 2, rows, cz), f32),
+                pltpu.VMEM((1, 2, rows, cz), f32),
                 pltpu.SemaphoreType.DMA((2, nmsg)),
                 pltpu.SemaphoreType.DMA((2, nmsg)),
             ],
             compiler_params=pltpu.CompilerParams(
-                collective_id=0, has_side_effects=True, vmem_limit_bytes=48 * 1024 * 1024
+                collective_id=0, has_side_effects=True, vmem_limit_bytes=67043328
             ),
         )(adj, rho, vel, mask)
+        out, sens = pl.pallas_call(
+            functools.partial(_last, dims),
+            out_shape=(
+                jax.ShapeDtypeStruct((npop, rows, cz), f32),
+                jax.ShapeDtypeStruct((rows, cz), f32),
+            ),
+            in_specs=[hbm] * 9,
+            out_specs=(hbm, hbm),
+            scratch_shapes=[
+                pltpu.VMEM((npop, rows, cz), f32),
+                pltpu.VMEM((rows, cz), f32),
+                pltpu.VMEM((1, 2, 5, cy, cz), f32),
+                pltpu.VMEM((1, 2, 5, cx, cz), f32),
+                pltpu.VMEM((1, 4, 8, cz), f32),
+                pltpu.VMEM((2, rows, cz), f32),
+                pltpu.VMEM((1, 2, rows, cz), f32),
+                pltpu.VMEM((1, rows, cz), f32),
+                pltpu.VMEM((1, 3, rows, cz), f32),
+                pltpu.VMEM((rows, cz), jnp.int32),
+                pltpu.VMEM((npop, rows, cz), f32),
+                pltpu.VMEM((rows, cz), f32),
+                pltpu.SemaphoreType.DMA((9,)),
+                pltpu.SemaphoreType.DMA((cx + 1,)),
+            ],
+            compiler_params=pltpu.CompilerParams(vmem_limit_bytes=67043328),
+        )(mid, s1, xh2, yh2, exy2, mh2, rho, vel, mask)
         return out.reshape(npop, cx, cy, cz), sens.reshape(cx, cy, cz)
 
     placed = (

time: 28.3 us -> 24.6 us (0.87)
  local copies, waits for them, and re-layouts: 5.69 us -> 0 us
  Pallas kernels: 21.7 us -> 23.9 us
    unnamed x10 -> x0, local copies, waits for them, and re-layouts: 5.69 us -> none
    pallas_call x1 -> x2, Pallas kernels: 21.7 us -> 23.9 us  [the longest x1 20.5 us: shards(): pl.pallas_call(functools.partial(_kernel, dims), out_shape=(jax.ShapeDtyp...]
where the time goes in v8:
time: 24.6 us; the launch traced here: 24.5 us
  Pallas kernels  23.9 us (97%)
  between operations  0.64 us (3%)
    pallas_call x1, Pallas kernels, shards(): pl.pallas_call(functools.partial(_kernel, dims), out_shape=(jax.ShapeDtyp...  20.5 us
    pallas_call x1, Pallas kernels, shards(): pl.pallas_call(functools.partial(_last, dims), out_shape=(jax.ShapeDtypeS...  3.32 us

profile of v8, /device:TPU:24, one launch (start us, length us, event | category | flops | bytes accessed | tf_op | source)
XLA Modules:
  0.0 24.5 jit_solution(9177498694798579073)
XLA Ops:
  0.6 20.5 %shard_map.59 = (f32[19,128,128]{2,1,0:T(8,128)}, f32[128,128]{1,0:T(8,128)}, f32[2,5,16,128]{3,2,1,0:T(8,128)}, f32[2,5,8,128]{3,2,1,0:T(8,128)}, f32[4,8,128]{2,1,0:T(8,128)}, /*index=5*/f32[2,128,128]{2,1,0:T(8,128)}) custom-call(f32[19,128,128]{2,1,0:T(8,128)} %bitcast.8, f32[2,128,128]{2,1,0:T(8,128)} %bitcast.9, f32[2,3,128,128]{3,2,1,0:T(8,128)} %bitcast.6, ...), custom_call_target="tpu_custom_call" | custom-call | tf_op jit(solution)/shard_map/pallas_call | solution.py:451
  21.2 3.3 %shard_map.60 = (f32[19,128,128]{2,1,0:T(8,128)}, f32[128,128]{1,0:T(8,128)}) custom-call(f32[19,128,128]{2,1,0:T(8,128)} %get-tuple-element.10.mid_hbm, f32[128,128]{1,0:T(8,128)} %get-tuple-element.11.s1_hbm, f32[2,5,16,128]{3,2,1,0:T(8,128)} %get-tuple-element.12.xh_hbm, f32[2,5,8,128]{3,2,1,0:T(8,128)} %get-tuple-element.13.yh_hbm, ...), custom_call_target="tpu_custom_call" | custom-call | tf_op jit(solution)/shard_map/pallas_call | solution.py:483

commit v9 on v8

--- a/solution.py
+++ b/solution.py
@@ -397,9 +397,15 @@
         pltpu.make_async_copy(vel_hbm.at[pl.ds(0, 1)], vel, in_sem.at[5]),
         pltpu.make_async_copy(mask_hbm, mask, in_sem.at[6]),
         pltpu.make_async_copy(s1_hbm, s1, in_sem.at[7]),
-        pltpu.make_async_copy(mid_hbm, mid, in_sem.at[8]),
+    ]
+    planes = [
+        pltpu.make_async_copy(mid_hbm.at[:, pl.ds(p * cy, cy), :], mid.at[:, pl.ds(p * cy, cy), :],
+                              in_sem.at[8 + p])
+        for p in range(cx)
     ]
     for copy in loads:
+        copy.start()
+    for copy in planes:
         copy.start()
     for copy in loads:
         copy.wait()
@@ -417,8 +423,15 @@
             fin[i, rs, :] = layers[i]
         sfin[rs, :] = s1[rs, :] + sens
 
-    _step(0, mid, xh, yh, exy, mt, rho, vel, mask, 0, emit,
-          before=lambda p: flush(p - 1) if p >= 1 else None)
+    def before(p):
+        if p == 0:
+            planes[0].wait()
+        if p + 1 < cx:
+            planes[p + 1].wait()
+        if p >= 1:
+            flush(p - 1)
+
+    _step(0, mid, xh, yh, exy, mt, rho, vel, mask, 0, emit, before=before)
     flush(cx - 1)
     sens_copy = pltpu.make_async_copy(sfin, sens_hbm, out_sem.at[cx])
     sens_copy.start()
@@ -501,7 +514,7 @@
                 pltpu.VMEM((rows, cz), jnp.int32),
                 pltpu.VMEM((npop, rows, cz), f32),
                 pltpu.VMEM((rows, cz), f32),
-                pltpu.SemaphoreType.DMA((9,)),
+                pltpu.SemaphoreType.DMA((8 + cx,)),
                 pltpu.SemaphoreType.DMA((cx + 1,)),
             ],
             compiler_params=pltpu.CompilerParams(vmem_limit_bytes=67043328),

time: 24.6 us -> 24.8 us (level)
  no operation moved by 1% of the time
where the time goes in v9:
time: 24.8 us; the launch traced here: 24.7 us
  Pallas kernels  24 us (97%)
  between operations  0.64 us (3%)
    pallas_call x1, Pallas kernels, shards(): pl.pallas_call(functools.partial(_kernel, dims), out_shape=(jax.ShapeDtyp...  20.5 us
    pallas_call x1, Pallas kernels, shards(): pl.pallas_call(functools.partial(_last, dims), out_shape=(jax.ShapeDtypeS...  3.47 us

profile of v9, /device:TPU:24, one launch (start us, length us, event | category | flops | bytes accessed | tf_op | source)
XLA Modules:
  0.0 24.7 jit_solution(9666927404046005977)
XLA Ops:
  0.6 20.5 %shard_map.59 = (f32[19,128,128]{2,1,0:T(8,128)}, f32[128,128]{1,0:T(8,128)}, f32[2,5,16,128]{3,2,1,0:T(8,128)}, f32[2,5,8,128]{3,2,1,0:T(8,128)}, f32[4,8,128]{2,1,0:T(8,128)}, /*index=5*/f32[2,128,128]{2,1,0:T(8,128)}) custom-call(f32[19,128,128]{2,1,0:T(8,128)} %bitcast.8, f32[2,128,128]{2,1,0:T(8,128)} %bitcast.9, f32[2,3,128,128]{3,2,1,0:T(8,128)} %bitcast.6, ...), custom_call_target="tpu_custom_call" | custom-call | tf_op jit(solution)/shard_map/pallas_call | solution.py:464
  21.2 3.5 %shard_map.60 = (f32[19,128,128]{2,1,0:T(8,128)}, f32[128,128]{1,0:T(8,128)}) custom-call(f32[19,128,128]{2,1,0:T(8,128)} %get-tuple-element.10.mid_hbm, f32[128,128]{1,0:T(8,128)} %get-tuple-element.11.s1_hbm, f32[2,5,16,128]{3,2,1,0:T(8,128)} %get-tuple-element.12.xh_hbm, f32[2,5,8,128]{3,2,1,0:T(8,128)} %get-tuple-element.13.yh_hbm, ...), custom_call_target="tpu_custom_call" | custom-call | tf_op jit(solution)/shard_map/pallas_call | solution.py:496

commit v10 on v8

--- a/solution.py
+++ b/solution.py
@@ -368,11 +368,11 @@
 
     _step(0, adj_ref, xh, yh, exy, mt, rho_ref, vel_ref, mask_ref, 1, emit,
           before=lambda p: flush(p - 1) if p >= 1 else None)
+    prepare(1, mid)
+    send(1, mid)
     flush(cx - 1)
     sens_copy = pltpu.make_async_copy(sfin, sens_out, out_sem.at[cx])
     sens_copy.start()
-    prepare(1, mid)
-    send(1, mid)
     finish(1, mid)
     for p in range(cx):
         rs = pl.ds(p * cy, cy)

time: 24.6 us -> 24.6 us (level)
  no operation moved by 1% of the time
where the time goes in v10:
time: 24.6 us; the launch traced here: 24.5 us
  Pallas kernels  23.9 us (97%)
  between operations  0.64 us (3%)
    pallas_call x1, Pallas kernels, shards(): pl.pallas_call(functools.partial(_kernel, dims), out_shape=(jax.ShapeDtyp...  20.5 us
    pallas_call x1, Pallas kernels, shards(): pl.pallas_call(functools.partial(_last, dims), out_shape=(jax.ShapeDtypeS...  3.32 us

profile of v10, /device:TPU:24, one launch (start us, length us, event | category | flops | bytes accessed | tf_op | source)
XLA Modules:
  0.0 24.5 jit_solution(17593622743001167438)
XLA Ops:
  0.6 20.5 %shard_map.59 = (f32[19,128,128]{2,1,0:T(8,128)}, f32[128,128]{1,0:T(8,128)}, f32[2,5,16,128]{3,2,1,0:T(8,128)}, f32[2,5,8,128]{3,2,1,0:T(8,128)}, f32[4,8,128]{2,1,0:T(8,128)}, /*index=5*/f32[2,128,128]{2,1,0:T(8,128)}) custom-call(f32[19,128,128]{2,1,0:T(8,128)} %bitcast.8, f32[2,128,128]{2,1,0:T(8,128)} %bitcast.9, f32[2,3,128,128]{3,2,1,0:T(8,128)} %bitcast.6, ...), custom_call_target="tpu_custom_call" | custom-call | tf_op jit(solution)/shard_map/pallas_call | solution.py:451
  21.2 3.3 %shard_map.60 = (f32[19,128,128]{2,1,0:T(8,128)}, f32[128,128]{1,0:T(8,128)}) custom-call(f32[19,128,128]{2,1,0:T(8,128)} %get-tuple-element.10.mid_hbm, f32[128,128]{1,0:T(8,128)} %get-tuple-element.11.s1_hbm, f32[2,5,16,128]{3,2,1,0:T(8,128)} %get-tuple-element.12.xh_hbm, f32[2,5,8,128]{3,2,1,0:T(8,128)} %get-tuple-element.13.yh_hbm, ...), custom_call_target="tpu_custom_call" | custom-call | tf_op jit(solution)/shard_map/pallas_call | solution.py:483

commit v11 on v10

--- a/solution.py
+++ b/solution.py
@@ -94,14 +94,34 @@
 
 
 def _collide(pulled, rho, ux, uy, uz, fluid):
-    p0 = _comb(pulled, lambda c: 1)
-    p1 = [_comb(pulled, lambda c, a=a: c[a]) for a in range(3)]
+    u = (ux, uy, uz)
+    pair = {i: pulled[i] + pulled[i + 1] for i in range(1, 19, 2)}
+    diff = {i: pulled[i] - pulled[i + 1] for i in range(1, 19, 2)}
+    w1, w2 = 1.0 / 18.0, 1.0 / 36.0
+
+    def signed(terms, table):
+        total = None
+        for i, sgn in terms:
+            v = table[i]
+            if total is None:
+                total = v if sgn > 0 else -v
+            else:
+                total = total + v if sgn > 0 else total - v
+        return total
+
+    edges = [i for i in range(7, 19, 2)]
+    p0 = pulled[0] * (1.0 / 3.0) + (pair[1] + pair[3] + pair[5]) * w1 + signed([(i, 1) for i in edges], pair) * w2
+    p1 = []
     q = {}
+    for a, axis_pop in enumerate((1, 3, 5)):
+        edge = [i for i in edges if VELOCITIES[i][a] != 0]
+        p1.append(diff[axis_pop] * w1 + signed([(i, VELOCITIES[i][a]) for i in edge], diff) * w2)
+        q[a, a] = pair[axis_pop] * w1 + signed([(i, 1) for i in edge], pair) * w2
     for a in range(3):
-        for b in range(a, 3):
-            q[a, b] = _comb(pulled, lambda c, a=a, b=b: c[a] * c[b])
+        for b in range(a + 1, 3):
+            edge = [i for i in edges if VELOCITIES[i][a] != 0 and VELOCITIES[i][b] != 0]
+            q[a, b] = signed([(i, VELOCITIES[i][a] * VELOCITIES[i][b]) for i in edge], pair) * w2
             q[b, a] = q[a, b]
-    u = (ux, uy, uz)
     usq = ux * ux + uy * uy + uz * uz
     qu = [q[a, 0] * ux + q[a, 1] * uy + q[a, 2] * uz for a in range(3)]
     p1u = p1[0] * ux + p1[1] * uy + p1[2] * uz
@@ -117,7 +137,6 @@
     layers = []
     for i in range(19):
         c = VELOCITIES[i]
-        key = tuple(c)
         terms = [(a, c[a]) for a in range(3) if c[a] != 0]
         cv = None
         if terms:
@@ -145,9 +164,9 @@
                 along = u[a] if c[a] > 0 else -u[a]
             else:
                 along = along + u[a] if c[a] > 0 else along - u[a]
-        term = (6.0 * WEIGHTS[i]) * along * (pulled[OPPOSITE[i]] - pulled[i])
+        term = (6.0 * WEIGHTS[i]) * along * diff[i]
         sens = term if sens is None else sens + term
-    sens = jnp.where(fluid, rho * sens, 0.0)
+    sens = jnp.where(fluid, -(rho * sens), 0.0)
     return layers, sens
 
 

time: 24.6 us -> 24.6 us (level)
  no operation moved by 1% of the time
where the time goes in v11:
time: 24.6 us; the launch traced here: 24.4 us
  Pallas kernels  23.8 us (97%)
  between operations  0.64 us (3%)
    pallas_call x1, Pallas kernels, shards(): pl.pallas_call(functools.partial(_kernel, dims), out_shape=(jax.ShapeDtyp...  20.5 us
    pallas_call x1, Pallas kernels, shards(): pl.pallas_call(functools.partial(_last, dims), out_shape=(jax.ShapeDtypeS...  3.29 us

profile of v11, /device:TPU:24, one launch (start us, length us, event | category | flops | bytes accessed | tf_op | source)
XLA Modules:
  0.0 24.4 jit_solution(13864337699788769367)
XLA Ops:
  0.6 20.5 %shard_map.59 = (f32[19,128,128]{2,1,0:T(8,128)}, f32[128,128]{1,0:T(8,128)}, f32[2,5,16,128]{3,2,1,0:T(8,128)}, f32[2,5,8,128]{3,2,1,0:T(8,128)}, f32[4,8,128]{2,1,0:T(8,128)}, /*index=5*/f32[2,128,128]{2,1,0:T(8,128)}) custom-call(f32[19,128,128]{2,1,0:T(8,128)} %bitcast.8, f32[2,128,128]{2,1,0:T(8,128)} %bitcast.9, f32[2,3,128,128]{3,2,1,0:T(8,128)} %bitcast.6, ...), custom_call_target="tpu_custom_call" | custom-call | tf_op jit(solution)/shard_map/pallas_call | solution.py:470
  21.1 3.3 %shard_map.60 = (f32[19,128,128]{2,1,0:T(8,128)}, f32[128,128]{1,0:T(8,128)}) custom-call(f32[19,128,128]{2,1,0:T(8,128)} %get-tuple-element.10.mid_hbm, f32[128,128]{1,0:T(8,128)} %get-tuple-element.11.s1_hbm, f32[2,5,16,128]{3,2,1,0:T(8,128)} %get-tuple-element.12.xh_hbm, f32[2,5,8,128]{3,2,1,0:T(8,128)} %get-tuple-element.13.yh_hbm, ...), custom_call_target="tpu_custom_call" | custom-call | tf_op jit(solution)/shard_map/pallas_call | solution.py:502

commit v12 on v11

--- a/solution.py
+++ b/solution.py
@@ -378,7 +378,7 @@
 
     def flush(p):
         rs = pl.ds(p * cy, cy)
-        pltpu.make_async_copy(mid.at[:, rs, :], mid_out.at[:, rs, :], out_sem.at[p]).start()
+        pltpu.make_async_copy(mid.at[:, rs, :], mid_out.at[p], out_sem.at[p]).start()
 
     def emit(p, rs, layers, sens):
         for i in range(19):
@@ -395,7 +395,7 @@
     finish(1, mid)
     for p in range(cx):
         rs = pl.ds(p * cy, cy)
-        pltpu.make_async_copy(mid.at[:, rs, :], mid_out.at[:, rs, :], out_sem.at[p]).wait()
+        pltpu.make_async_copy(mid.at[:, rs, :], mid_out.at[p], out_sem.at[p]).wait()
     sens_copy.wait()
 
 
@@ -416,9 +416,16 @@
         pltpu.make_async_copy(vel_hbm.at[pl.ds(0, 1)], vel, in_sem.at[5]),
         pltpu.make_async_copy(mask_hbm, mask, in_sem.at[6]),
         pltpu.make_async_copy(s1_hbm, s1, in_sem.at[7]),
-        pltpu.make_async_copy(mid_hbm, mid, in_sem.at[8]),
     ]
+    planes = [
+        pltpu.make_async_copy(mid_hbm.at[p], mid.at[:, pl.ds(p * cy, cy), :], in_sem.at[8 + p])
+        for p in range(cx)
+    ]
+    for copy in planes[:2]:
+        copy.start()
     for copy in loads:
+        copy.start()
+    for copy in planes[2:]:
         copy.start()
     for copy in loads:
         copy.wait()
@@ -436,8 +443,15 @@
             fin[i, rs, :] = layers[i]
         sfin[rs, :] = s1[rs, :] + sens
 
-    _step(0, mid, xh, yh, exy, mt, rho, vel, mask, 0, emit,
-          before=lambda p: flush(p - 1) if p >= 1 else None)
+    def before(p):
+        if p == 0:
+            planes[0].wait()
+        if p + 1 < cx:
+            planes[p + 1].wait()
+        if p >= 1:
+            flush(p - 1)
+
+    _step(0, mid, xh, yh, exy, mt, rho, vel, mask, 0, emit, before=before)
     flush(cx - 1)
     sens_copy = pltpu.make_async_copy(sfin, sens_hbm, out_sem.at[cx])
     sens_copy.start()
@@ -470,7 +484,7 @@
         mid, s1, xh2, yh2, exy2, mh2 = pl.pallas_call(
             functools.partial(_kernel, dims),
             out_shape=(
-                jax.ShapeDtypeStruct((npop, rows, cz), f32),
+                jax.ShapeDtypeStruct((cx, npop, cy, cz), f32),
                 jax.ShapeDtypeStruct((rows, cz), f32),
             ) + halo_shapes,
             in_specs=[hbm] * 4,
@@ -520,7 +534,7 @@
                 pltpu.VMEM((rows, cz), jnp.int32),
                 pltpu.VMEM((npop, rows, cz), f32),
                 pltpu.VMEM((rows, cz), f32),
-                pltpu.SemaphoreType.DMA((9,)),
+                pltpu.SemaphoreType.DMA((8 + cx,)),
                 pltpu.SemaphoreType.DMA((cx + 1,)),
             ],
             compiler_params=pltpu.CompilerParams(vmem_limit_bytes=67043328),

time: 24.6 us -> 24.8 us (level)
  no operation moved by 1% of the time
where the time goes in v12:
time: 24.8 us; the launch traced here: 24.6 us
  Pallas kernels  24 us (97%)
  between operations  0.64 us (3%)
    pallas_call x1, Pallas kernels, shards(): pl.pallas_call(functools.partial(_kernel, dims), out_shape=(jax.ShapeDtyp...  20.5 us
    pallas_call x1, Pallas kernels, shards(): pl.pallas_call(functools.partial(_last, dims), out_shape=(jax.ShapeDtypeS...  3.51 us

profile of v12, /device:TPU:24, one launch (start us, length us, event | category | flops | bytes accessed | tf_op | source)
XLA Modules:
  0.0 24.6 jit_solution(18153686670913484404)
XLA Ops:
  0.6 20.5 %shard_map.59 = (f32[8,19,16,128]{3,2,1,0:T(8,128)}, f32[128,128]{1,0:T(8,128)}, f32[2,5,16,128]{3,2,1,0:T(8,128)}, f32[2,5,8,128]{3,2,1,0:T(8,128)}, f32[4,8,128]{2,1,0:T(8,128)}, /*index=5*/f32[2,128,128]{2,1,0:T(8,128)}) custom-call(f32[19,128,128]{2,1,0:T(8,128)} %bitcast.8, f32[2,128,128]{2,1,0:T(8,128)} %bitcast.9, f32[2,3,128,128]{3,2,1,0:T(8,128)} %bitcast.6, ...), custom_call_target="tpu_custom_call" | custom-call | tf_op jit(solution)/shard_map/pallas_call | solution.py:484
  21.1 3.5 %shard_map.60 = (f32[19,128,128]{2,1,0:T(8,128)}, f32[128,128]{1,0:T(8,128)}) custom-call(f32[8,19,16,128]{3,2,1,0:T(8,128)} %get-tuple-element.10.mid_hbm, f32[128,128]{1,0:T(8,128)} %get-tuple-element.11.s1_hbm, f32[2,5,16,128]{3,2,1,0:T(8,128)} %get-tuple-element.12.xh_hbm, f32[2,5,8,128]{3,2,1,0:T(8,128)} %get-tuple-element.13.yh_hbm, ...), custom_call_target="tpu_custom_call" | custom-call | tf_op jit(solution)/shard_map/pallas_call | solution.py:516

commit v13 on v11

--- a/solution.py
+++ b/solution.py
@@ -436,14 +436,12 @@
             fin[i, rs, :] = layers[i]
         sfin[rs, :] = s1[rs, :] + sens
 
-    _step(0, mid, xh, yh, exy, mt, rho, vel, mask, 0, emit,
-          before=lambda p: flush(p - 1) if p >= 1 else None)
-    flush(cx - 1)
+    _step(0, mid, xh, yh, exy, mt, rho, vel, mask, 0, emit)
+    whole = pltpu.make_async_copy(fin, out_hbm, out_sem.at[0])
+    whole.start()
     sens_copy = pltpu.make_async_copy(sfin, sens_hbm, out_sem.at[cx])
     sens_copy.start()
-    for p in range(cx):
-        rs = pl.ds(p * cy, cy)
-        pltpu.make_async_copy(fin.at[:, rs, :], out_hbm.at[:, rs, :], out_sem.at[p]).wait()
+    whole.wait()
     sens_copy.wait()
 
 

time: 24.6 us -> 24.9 us (1.012)
  Pallas kernels: 23.8 us -> 24.1 us
    pallas_call x1, Pallas kernels: 3.29 us -> 3.65 us  [shards(): pl.pallas_call(functools.partial(_last, dims), out_shape=(jax.ShapeDtypeS...]
where the time goes in v13:
time: 24.9 us; the launch traced here: 24.8 us
  Pallas kernels  24.1 us (97%)
  between operations  0.64 us (3%)
    pallas_call x1, Pallas kernels, shards(): pl.pallas_call(functools.partial(_kernel, dims), out_shape=(jax.ShapeDtyp...  20.5 us
    pallas_call x1, Pallas kernels, shards(): pl.pallas_call(functools.partial(_last, dims), out_shape=(jax.ShapeDtypeS...  3.65 us

profile of v13, /device:TPU:24, one launch (start us, length us, event | category | flops | bytes accessed | tf_op | source)
XLA Modules:
  0.0 24.8 jit_solution(11704143382639355816)
XLA Ops:
  0.6 20.5 %shard_map.59 = (f32[19,128,128]{2,1,0:T(8,128)}, f32[128,128]{1,0:T(8,128)}, f32[2,5,16,128]{3,2,1,0:T(8,128)}, f32[2,5,8,128]{3,2,1,0:T(8,128)}, f32[4,8,128]{2,1,0:T(8,128)}, /*index=5*/f32[2,128,128]{2,1,0:T(8,128)}) custom-call(f32[19,128,128]{2,1,0:T(8,128)} %bitcast.8, f32[2,128,128]{2,1,0:T(8,128)} %bitcast.9, f32[2,3,128,128]{3,2,1,0:T(8,128)} %bitcast.6, ...), custom_call_target="tpu_custom_call" | custom-call | tf_op jit(solution)/shard_map/pallas_call | solution.py:468
  21.1 3.7 %shard_map.60 = (f32[19,128,128]{2,1,0:T(8,128)}, f32[128,128]{1,0:T(8,128)}) custom-call(f32[19,128,128]{2,1,0:T(8,128)} %get-tuple-element.10.mid_hbm, f32[128,128]{1,0:T(8,128)} %get-tuple-element.11.s1_hbm, f32[2,5,16,128]{3,2,1,0:T(8,128)} %get-tuple-element.12.xh_hbm, f32[2,5,8,128]{3,2,1,0:T(8,128)} %get-tuple-element.13.yh_hbm, ...), custom_call_target="tpu_custom_call" | custom-call | tf_op jit(solution)/shard_map/pallas_call | solution.py:500

commit v14 on v11

--- a/solution.py
+++ b/solution.py
@@ -420,12 +420,14 @@
     ]
     for copy in loads:
         copy.start()
-    for copy in loads:
+    for copy in loads[:4]:
         copy.wait()
     _zero_missing(exists, xh.at[0], yh.at[0], exy.at[0], mh)
 
     for side in range(2):
         mt[0, side] = mh[side].T
+    for copy in loads[4:]:
+        copy.wait()
 
     def flush(p):
         rs = pl.ds(p * cy, cy)

time: 24.6 us -> 24.5 us (level)
  no operation moved by 1% of the time
where the time goes in v14:
time: 24.5 us; the launch traced here: 24.3 us
  Pallas kernels  23.7 us (97%)
  between operations  0.64 us (3%)
    pallas_call x1, Pallas kernels, shards(): pl.pallas_call(functools.partial(_kernel, dims), out_shape=(jax.ShapeDtyp...  20.5 us
    pallas_call x1, Pallas kernels, shards(): pl.pallas_call(functools.partial(_last, dims), out_shape=(jax.ShapeDtypeS...  3.21 us

profile of v14, /device:TPU:24, one launch (start us, length us, event | category | flops | bytes accessed | tf_op | source)
XLA Modules:
  0.0 24.3 jit_solution(6452195843633282680)
XLA Ops:
  0.6 20.5 %shard_map.59 = (f32[19,128,128]{2,1,0:T(8,128)}, f32[128,128]{1,0:T(8,128)}, f32[2,5,16,128]{3,2,1,0:T(8,128)}, f32[2,5,8,128]{3,2,1,0:T(8,128)}, f32[4,8,128]{2,1,0:T(8,128)}, /*index=5*/f32[2,128,128]{2,1,0:T(8,128)}) custom-call(f32[19,128,128]{2,1,0:T(8,128)} %bitcast.8, f32[2,128,128]{2,1,0:T(8,128)} %bitcast.9, f32[2,3,128,128]{3,2,1,0:T(8,128)} %bitcast.6, ...), custom_call_target="tpu_custom_call" | custom-call | tf_op jit(solution)/shard_map/pallas_call | solution.py:472
  21.1 3.2 %shard_map.60 = (f32[19,128,128]{2,1,0:T(8,128)}, f32[128,128]{1,0:T(8,128)}) custom-call(f32[19,128,128]{2,1,0:T(8,128)} %get-tuple-element.10.mid_hbm, f32[128,128]{1,0:T(8,128)} %get-tuple-element.11.s1_hbm, f32[2,5,16,128]{3,2,1,0:T(8,128)} %get-tuple-element.12.xh_hbm, f32[2,5,8,128]{3,2,1,0:T(8,128)} %get-tuple-element.13.yh_hbm, ...), custom_call_target="tpu_custom_call" | custom-call | tf_op jit(solution)/shard_map/pallas_call | solution.py:504
